TPU v7x, 128 devices: a whole 4x4x4 slice. The times are simulated.
128 devices in a mesh: owner: 32 (over x, z, core), view: 4 (over y).
Axes of the slice: x: 4, y: 4, z: 4, core: 2. Of those that a mesh axis runs over, the one named last changes fastest.
Arguments:
- estimate: float32 [512, 128, 512], P('owner'), may hold values from 0.5 to 2
- axial_views: float32 [4, 512, 128, 512], P('view', 'owner'), may hold values from 0.3 to 3
- lateral_views: float32 [4, 512, 128, 512], P('view', 'owner'), may hold values from 0.3 to 3
- psf_axial: float32 [4, 3, 33], P('view'), may hold values from 0.05 to 1
- psf_lateral: float32 [4, 3, 33], P('view'), may hold values from 0.05 to 1
- coverage: int32 [32, 4, 8], P('owner'), may hold values from 0 to 1, as said below
Outputs:
- deconvolved: float32 [512, 128, 512], P('owner')
Inputs may be any that keep to these rules, and one draw needn't show every extreme that they name: `coverage`: each block is covered by 2 to 6 views; some block by exactly 6 and some by exactly 2.
All inputs are finite; a program needn't handle non-finite values.
Results may differ from a plain program's by a relative error of at most 0.0001.
Values sent between devices are 32-bit elements; how exact they have to be, the bound alone decides.
No kernel may reach another device: no remote copies, remote signals or barrier semaphores. Data moves between devices by JAX's collectives and lax.ppermute only.
A program may use at most 128 MiB of HBM per device.

v0:
```python
import jax
import jax.numpy as jnp
from jax import lax
from jax.sharding import PartitionSpec as P

VA = 4
ITERS = 2


PRECISE = lax.Precision.HIGHEST


def extended(shard, sides, width):
    for axis, dim in sides:
        peers, length = (lax.axis_size(axis), shard.shape[dim])
        up = [(i, (i + 1) % peers) for i in range(peers - 1)]
        down = [(j, i) for i, j in up]
        last = lax.slice_in_dim(shard, length - width, length, axis=dim)
        leading = lax.slice_in_dim(shard, 0, width, axis=dim)
        before = lax.ppermute(last, axis, up)
        after = lax.ppermute(leading, axis, down)
        shard = jnp.concatenate([before, shard, after], axis=dim)
    return shard


def band_matrix(kernel, block_width):
    rim_width = (kernel.shape[-1] - 1) // 2
    row_index = jnp.arange(block_width + 2 * rim_width)[:, None]
    col_index = jnp.arange(block_width)[None, :]
    matches = (row_index - col_index)[:, :, None] == jnp.arange(kernel.shape[-1])[None, None, :]
    return jnp.sum(jnp.where(matches[None], kernel[:, None, None, :], 0.0), axis=-1)


def middle_matrix(kernel, length):
    rim_width = (kernel.shape[-1] - 1) // 2
    row_index = jnp.arange(length)[:, None]
    col_index = jnp.arange(length)[None, :]
    matches = (row_index - col_index + rim_width)[:, :, None] == jnp.arange(kernel.shape[-1])[
        None, None, :
    ]
    return jnp.sum(jnp.where(matches[None], kernel[:, None, None, :], 0.0), axis=-1)


def along_last(volume, kernel):
    rim_width = (kernel.shape[-1] - 1) // 2
    length = volume.shape[-1]
    block_width = min(128, length)
    blocks = volume.reshape(volume.shape[:-1] + (length // block_width, block_width))
    zero_rim = jnp.zeros(blocks.shape[:-2] + (1, rim_width), volume.dtype)
    left_rim = jnp.concatenate([zero_rim, blocks[..., :-1, block_width - rim_width :]], axis=-2)
    right_rim = jnp.concatenate([blocks[..., 1:, :rim_width], zero_rim], axis=-2)
    windows = jnp.concatenate([left_rim, blocks, right_rim], axis=-1)
    result = jnp.einsum(
        "vabns,vsi->vabni", windows, band_matrix(kernel, block_width), precision=PRECISE
    )
    return result.reshape(volume.shape)


def forward(padded, kernel_first, kernel_mid, kernel_last):
    plane_count = padded.shape[0] - (kernel_first.shape[-1] - 1)
    result = jnp.einsum(
        "syl,vsi->viyl", padded, band_matrix(kernel_first, plane_count), precision=PRECISE
    )
    result = jnp.einsum(
        "viyl,vyk->vikl", result, middle_matrix(kernel_mid, result.shape[2]), precision=PRECISE
    )
    return along_last(result, kernel_last)


def backward(padded, kernel_first, kernel_mid, kernel_last):
    plane_count = padded.shape[1] - (kernel_first.shape[-1] - 1)
    result = jnp.einsum(
        "vsyl,vsi->viyl", padded, band_matrix(kernel_first, plane_count), precision=PRECISE
    )
    result = jnp.einsum(
        "viyl,vyk->vikl", result, middle_matrix(kernel_mid, result.shape[2]), precision=PRECISE
    )
    return along_last(result, kernel_last)


def edge_weights(kernel, positions, length):
    rim_width = (kernel.shape[-1] - 1) // 2
    source = positions[:, None] + jnp.arange(kernel.shape[-1])[None, :] - rim_width
    inside = (source >= 0) & (source < length)
    return jnp.sum(jnp.where(inside[None], kernel[:, None, :], 0.0), axis=-1)


def log_correction(padded, kernel_first, kernel_mid, kernel_last, first_start, first_total):
    back_sum = backward(padded, kernel_first, kernel_mid, kernel_last)
    plane_count, line_count, column_count = back_sum.shape[1:]
    first_weights = edge_weights(kernel_first, first_start + jnp.arange(plane_count), first_total)
    mid_weights = edge_weights(kernel_mid, jnp.arange(line_count), line_count)
    last_weights = edge_weights(kernel_last, jnp.arange(column_count), column_count)
    scale_sum = (
        first_weights[:, :, None, None]
        * mid_weights[:, None, :, None]
        * last_weights[:, None, None, :]
    )
    return jnp.log(back_sum / scale_sum)


def select_views(covered, view_ids):
    picked = (jnp.arange(covered.shape[-1])[None, :] == view_ids[:, None]).astype(jnp.float32)
    return jnp.einsum("vw,xw->vx", picked, covered, precision=PRECISE)


def slab_logs(padded_estimate, view_data, kernel, flipped, weights, first_start, first_total):
    blurred = forward(padded_estimate, kernel[:, 0], kernel[:, 1], kernel[:, 2])
    quotient = view_data / blurred
    rim_width = (kernel.shape[-1] - 1) // 2
    quotient_padded = extended(quotient, (("owner", 1),), rim_width)
    log_terms = log_correction(
        quotient_padded, flipped[:, 0], flipped[:, 1], flipped[:, 2], first_start, first_total
    )
    return jnp.sum(weights[:, None, None, :] * log_terms, axis=0)


def local(estimate, axial_views, lateral_views, psf_axial, psf_lateral, coverage):
    plane_count, line_count, column_count = estimate.shape
    owners = lax.axis_size("owner")
    slab_index = lax.axis_index("owner")
    view_index = lax.axis_index("view")
    slab_width = column_count // owners
    rim_width = (psf_axial.shape[-1] - 1) // 2
    kernel_axial = psf_axial / jnp.sum(psf_axial, axis=-1, keepdims=True)
    kernel_lateral = psf_lateral / jnp.sum(psf_lateral, axis=-1, keepdims=True)
    flipped_axial = kernel_axial[..., ::-1]
    flipped_lateral = kernel_lateral[..., ::-1]
    block_width = column_count // coverage.shape[1]
    covered = jnp.repeat(coverage[0].astype(jnp.float32), block_width, axis=0)
    cover_count = jnp.sum(covered, axis=-1)
    axial_count = psf_axial.shape[0]
    lateral_count = psf_lateral.shape[0]
    weights_axial = select_views(covered, view_index * axial_count + jnp.arange(axial_count))
    weights_lateral = select_views(
        covered, VA + view_index * lateral_count + jnp.arange(lateral_count)
    )
    plane_start = slab_index * plane_count
    plane_total = plane_count * owners
    for iteration in range(ITERS):
        padded_estimate = extended(estimate, (("owner", 0),), rim_width)
        log_total = slab_logs(
            padded_estimate,
            axial_views,
            kernel_axial,
            flipped_axial,
            weights_axial,
            plane_start,
            plane_total,
        )
        spread = estimate.reshape(plane_count, line_count, owners, slab_width).transpose(3, 1, 2, 0)
        column = lax.all_to_all(spread, "owner", split_axis=2, concat_axis=3, tiled=True).reshape(
            slab_width, line_count, plane_total
        )
        column_padded = extended(column, (("owner", 0),), rim_width)
        blurred = forward(
            column_padded, kernel_lateral[:, 2], kernel_lateral[:, 1], kernel_lateral[:, 0]
        )
        quotient = lateral_views / blurred
        quotient_padded = extended(quotient, (("owner", 1),), rim_width)
        log_terms = log_correction(
            quotient_padded,
            flipped_lateral[:, 2],
            flipped_lateral[:, 1],
            flipped_lateral[:, 0],
            slab_index * slab_width,
            column_count,
        )
        turned = log_terms.reshape(
            lateral_count, slab_width, line_count, owners, plane_count
        ).transpose(0, 4, 2, 3, 1)
        slab_terms = lax.all_to_all(
            turned, "owner", split_axis=3, concat_axis=4, tiled=True
        ).reshape(lateral_count, plane_count, line_count, column_count)
        log_total = log_total + jnp.sum(weights_lateral[:, None, None, :] * slab_terms, axis=0)
        log_total = lax.psum(log_total, "view")
        estimate = estimate * jnp.exp(log_total / cover_count[None, None, :])
    return estimate


def solution(mesh):
    in_specs = (
        P("owner", None, None),
        P("view", "owner", None, None),
        P("view", "owner", None, None),
        P("view", None, None),
        P("view", None, None),
        P("owner", None, None),
    )
    out_specs = P("owner", None, None)
    return jax.shard_map(local, mesh=mesh, in_specs=in_specs, out_specs=out_specs, check_vma=False)
```

profile of v0, /device:TPU:1, one launch (start us, length us, event | category | flops | bytes accessed | tf_op | source)
XLA Modules:
  0.0 909.1 jit_solution(11516271760494789973)
XLA Ops:
  6.5 5.3 copy.156
  14.6 59.9 %all_to_all.16 = f32[16,128,32,16]{1,0,3,2:T(8,128)} all-to-all(f32[16,128,32,16]{1,0,3,2:T(8,128)S(1)} %copy.157), channel_id=1, replica_groups=mesh['owner'=32,'view'=4] {'owner'}, dimensions={2} | all-to-all | bytes 8388608 | tf_op jit(solution)/shard_map/all_to_all | solution.py:152
  74.5 5.6 copy.159
  85.8 6.6 copy.177
  102.3 28.1 %collective-permute-done.5 = f32[16,128,512]{2,0,1:T(8,128)} collective-permute-done((f32[16,128,512]{2,0,1:T(8,128)}, f32[16,128,512]{2,0,1:T(8,128)}, u32[]{:S(2)}, u32[]{:S(2)}) %collective-permute-start.5) | collective-permute-done | bytes 4194336 | tf_op jit(solution)/shard_map/ppermute | solution.py:21
  131.6 9.0 fusion.11
  140.5 6.9 fusion.148
  147.5 5.3 copy.242
  154.0 8.3 fusion.70
  162.3 5.7 copy.168
  167.9 8.2 copy_divide_fusion.1
  183.1 8.8 fusion
  191.9 6.9 fusion.142
  198.8 5.3 copy.240
  205.3 8.3 fusion.80
  213.6 5.9 copy.149
  219.5 8.3 copy_divide_fusion.3
  233.4 8.8 fusion.17
  242.2 6.9 fusion.151
  249.2 5.3 copy.243
  255.7 5.9 fusion.65
  265.7 9.6 %all-to-all-start.1 = ((f32[1,16,128,32,16]{2,4,1,0,3:T(8,128)}), f32[1,16,128,32,16]{2,4,1,0,3:T(8,128)}, u32[]{:S(2)}, u32[]{:S(2)}) async-start(f32[1,16,128,32,16]{2,4,1,0,3:T(8,128)} %fusion.99), calls=%async_computation.1 | async-start | bytes 8388608 | tf_op jit(solution)/shard_map/all_to_all | solution.py:172
  278.5 9.6 %collective-permute-done.2 = f32[1,16,128,512]{3,1,2,0:T(8,128)} collective-permute-done((f32[1,16,128,512]{3,1,2,0:T(8,128)}, f32[1,16,128,512]{3,1,2,0:T(8,128)}, u32[]{:S(2)}, u32[]{:S(2)}) %collective-permute-start.2) | collective-permute-done | bytes 4194336 | tf_op jit(solution)/shard_map/ppermute | solution.py:20
  288.0 8.8 fusion.6
  296.8 6.9 fusion.145
  303.7 5.3 copy.241
  310.2 8.3 fusion.75
  318.6 5.5 copy.155
  324.1 5.3 all-to-all-done.1
  334.0 5.5 copy.176
  339.5 5.8 fusion.94
  345.5 100.3 %all-reduce.19.cloned.1.call-done = f32[16,128,512]{2,0,1:T(8,128)} async-done(((f32[16,128,512]{2,0,1:T(8,128)}), f32[16,128,512]{2,0,1:T(8,128)}) %all-reduce.19.cloned.1.call-update) | async-done | bytes 4194320 | tf_op jit(solution)/shard_map/psum | solution.py:176
  445.8 8.2 exponential_multiply_fusion.1
  454.0 5.3 copy.191
  462.1 58.4 %all_to_all.17 = f32[16,128,32,16]{1,0,3,2:T(8,128)} all-to-all(f32[16,128,32,16]{1,0,3,2:T(8,128)S(1)} %copy.192), channel_id=1, replica_groups=mesh['owner'=32,'view'=4] {'owner'}, dimensions={2} | all-to-all | bytes 8388608 | tf_op jit(solution)/shard_map/all_to_all | solution.py:152
  520.4 5.6 copy.194
  537.2 38.9 %collective-permute-done.13 = f32[16,128,512]{2,0,1:T(8,128)S(1)} collective-permute-done((f32[16,128,512]{2,0,1:T(8,128)}, f32[16,128,512]{2,0,1:T(8,128)S(1)}, u32[]{:S(2)}, u32[]{:S(2)}) %collective-permute-start.13) | collective-permute-done | bytes 4194336 | tf_op jit(solution)/shard_map/ppermute | solution.py:21
  577.3 7.9 fusion.33
  585.3 7.0 fusion.160
  592.3 5.3 copy.246
  598.8 8.3 fusion.50
  607.1 5.5 copy.203
  612.6 8.4 copy_divide_fusion
  627.2 8.8 fusion.22
  636.0 6.9 fusion.154
  642.9 5.3 copy.244
  649.4 8.3 fusion.60
  657.7 5.7 copy.184
  663.4 8.2 copy_divide_fusion.2
  677.2 8.8 fusion.39
  686.0 7.0 fusion.163
  693.0 5.3 copy.247
  699.5 5.9 fusion.45
  709.5 9.4 %all-to-all-start.3 = ((f32[1,16,128,32,16]{2,4,1,0,3:T(8,128)}), f32[1,16,128,32,16]{2,4,1,0,3:T(8,128)}, u32[]{:S(2)}, u32[]{:S(2)}) async-start(f32[1,16,128,32,16]{2,4,1,0,3:T(8,128)} %fusion.101), calls=%async_computation.3 | async-start | bytes 8388608 | tf_op jit(solution)/shard_map/all_to_all | solution.py:172
  722.4 9.3 %collective-permute-done.10 = f32[1,16,128,512]{3,1,2,0:T(8,128)} collective-permute-done((f32[1,16,128,512]{3,1,2,0:T(8,128)}, f32[1,16,128,512]{3,1,2,0:T(8,128)}, u32[]{:S(2)}, u32[]{:S(2)}) %collective-permute-start.10) | collective-permute-done | bytes 4194336 | tf_op jit(solution)/shard_map/ppermute | solution.py:20
  731.7 8.8 fusion.28
  740.5 6.9 fusion.157
  747.4 5.3 copy.245
  753.9 8.3 fusion.55
  762.2 5.5 copy.234
  767.7 6.0 all-to-all-done.3
  778.3 5.5 copy.211
  783.8 5.5 fusion.97
  789.4 103.7 %all-reduce.21.cloned.1.call-done = f32[16,128,512]{2,0,1:T(8,128)} async-done(((f32[16,128,512]{2,0,1:T(8,128)}), f32[16,128,512]{2,0,1:T(8,128)}) %all-reduce.21.cloned.1.call-update) | async-done | bytes 4194320 | tf_op jit(solution)/shard_map/psum | solution.py:176
  (88 shorter events, 101.3 us)
Async XLA Ops:
  80.1 18.6 %copy-start.3 = (f32[1,3,33]{2,0,1:T(1,128)S(1)}, f32[1,3,33]{2,0,1:T(1,128)}, u32[]{:S(2)}) copy-start(f32[1,3,33]{2,0,1:T(1,128)} %param.9) | copy-start | bytes 1192
  80.1 18.7 %copy-start.2 = (f32[1,3,33]{2,0,1:T(1,128)S(1)}, f32[1,3,33]{2,0,1:T(1,128)}, u32[]{:S(2)}) copy-start(f32[1,3,33]{2,0,1:T(1,128)} %param.10) | copy-start | bytes 1192
  80.1 50.3 %collective-permute-start.5 = (f32[16,128,512]{2,0,1:T(8,128)}, f32[16,128,512]{2,0,1:T(8,128)}, u32[]{:S(2)}, u32[]{:S(2)}) collective-permute-start(f32[16,128,512]{2,0,1:T(8,128)} %copy.159), channel_id=1, source_target_pairs={{4,0},{8,4},{12,8},{16,12},{20,16},{24,20},{28,24},{32,28},{36,32}... | collective-permute-start | bytes 12582920 | tf_op jit(solution)/shard_map/ppermute | solution.py:21
  82.3 49.3 %collective-permute-start.4 = (f32[16,128,512]{2,0,1:T(8,128)}, f32[16,128,512]{2,0,1:T(8,128)}, u32[]{:S(2)}, u32[]{:S(2)}) collective-permute-start(f32[16,128,512]{2,0,1:T(8,128)} %copy.159), channel_id=1, source_target_pairs={{0,4},{4,8},{8,12},{12,16},{16,20},{20,24},{24,28},{28,32},{32,36}... | collective-permute-start | bytes 12582920 | tf_op jit(solution)/shard_map/ppermute | solution.py:20
  92.5 90.6 %collective-permute-start = (f32[16,128,512]{2,0,1:T(8,128)}, f32[16,128,512]{2,0,1:T(8,128)}, u32[]{:S(2)}, u32[]{:S(2)}) collective-permute-start(f32[16,128,512]{2,0,1:T(8,128)} %copy.177), channel_id=1, source_target_pairs={{0,4},{4,8},{8,12},{12,16},{16,20},{20,24},{24,28},{28,32},{32,36}... | collective-permute-start | bytes 12582920 | tf_op jit(solution)/shard_map/ppermute | solution.py:20
  94.4 88.7 %collective-permute-start.1 = (f32[16,128,512]{2,0,1:T(8,128)}, f32[16,128,512]{2,0,1:T(8,128)}, u32[]{:S(2)}, u32[]{:S(2)}) collective-permute-start(f32[16,128,512]{2,0,1:T(8,128)} %copy.177), channel_id=1, source_target_pairs={{4,0},{8,4},{12,8},{16,12},{20,16},{24,20},{28,24},{32,28},{36,32}... | collective-permute-start | bytes 12582920 | tf_op jit(solution)/shard_map/ppermute | solution.py:21
  176.2 57.2 %collective-permute-start.7 = (f32[1,16,128,512]{3,1,2,0:T(8,128)}, f32[1,16,128,512]{3,1,2,0:T(8,128)}, u32[]{:S(2)}, u32[]{:S(2)}) collective-permute-start(f32[1,16,128,512]{3,1,2,0:T(8,128)} %copy_divide_fusion.1), channel_id=1, source_target_pairs={{4,0},{8,4},{12,8},{16,12},{20,16},{24,20},{28,24},{32,28},{36,32}... | collective-permute-start | bytes 12582920 | tf_op jit(solution)/shard_map/ppermute | solution.py:21
  178.1 55.3 %collective-permute-start.6 = (f32[1,16,128,512]{3,1,2,0:T(8,128)}, f32[1,16,128,512]{3,1,2,0:T(8,128)}, u32[]{:S(2)}, u32[]{:S(2)}) collective-permute-start(f32[1,16,128,512]{3,1,2,0:T(8,128)} %copy_divide_fusion.1), channel_id=1, source_target_pairs={{0,4},{4,8},{8,12},{12,16},{16,20},{20,24},{24,28},{28,32},{32,36}... | collective-permute-start | bytes 12582920 | tf_op jit(solution)/shard_map/ppermute | solution.py:20
  227.8 50.6 %collective-permute-start.3 = (f32[1,16,128,512]{3,1,2,0:T(8,128)}, f32[1,16,128,512]{3,1,2,0:T(8,128)}, u32[]{:S(2)}, u32[]{:S(2)}) collective-permute-start(f32[1,16,128,512]{3,1,2,0:T(8,128)} %copy_divide_fusion.3), channel_id=1, source_target_pairs={{4,0},{8,4},{12,8},{16,12},{20,16},{24,20},{28,24},{32,28},{36,32}... | collective-permute-start | bytes 12582920 | tf_op jit(solution)/shard_map/ppermute | solution.py:21
  229.8 58.3 %collective-permute-start.2 = (f32[1,16,128,512]{3,1,2,0:T(8,128)}, f32[1,16,128,512]{3,1,2,0:T(8,128)}, u32[]{:S(2)}, u32[]{:S(2)}) collective-permute-start(f32[1,16,128,512]{3,1,2,0:T(8,128)} %copy_divide_fusion.3), channel_id=1, source_target_pairs={{0,4},{4,8},{8,12},{12,16},{16,20},{20,24},{24,28},{28,32},{32,36}... | collective-permute-start | bytes 12582920 | tf_op jit(solution)/shard_map/ppermute | solution.py:20
  265.7 9.9 %copy-start.1 = (s32[1,4,8]{2,1,0:T(4,128)S(1)}, s32[1,4,8]{2,1,0:T(4,128)}, u32[]{:S(2)}) copy-start(s32[1,4,8]{2,1,0:T(4,128)} %param.11) | copy-start | bytes 388
  265.7 63.6 %all-to-all-start.1 = ((f32[1,16,128,32,16]{2,4,1,0,3:T(8,128)}), f32[1,16,128,32,16]{2,4,1,0,3:T(8,128)}, u32[]{:S(2)}, u32[]{:S(2)}) async-start(f32[1,16,128,32,16]{2,4,1,0,3:T(8,128)} %fusion.99), calls=%async_computation.1 | async-start | bytes 8388608 | tf_op jit(solution)/shard_map/all_to_all | solution.py:172
  275.3 170.5 %all-reduce.19.cloned.1.call-start = ((), (), s32[]{:S(2)}) async-start(), calls=%async_computation.4 | async-start | bytes 8388608 | tf_op jit(solution)/shard_map/psum | solution.py:176
  526.0 50.0 %collective-permute-start.13 = (f32[16,128,512]{2,0,1:T(8,128)}, f32[16,128,512]{2,0,1:T(8,128)S(1)}, u32[]{:S(2)}, u32[]{:S(2)}) collective-permute-start(f32[16,128,512]{2,0,1:T(8,128)} %copy.194), channel_id=1, source_target_pairs={{4,0},{8,4},{12,8},{16,12},{20,16},{24,20},{28,24},{32,28},{36,32}... | collective-permute-start | bytes 12582920 | tf_op jit(solution)/shard_map/ppermute | solution.py:21
  528.0 49.3 %collective-permute-start.12 = (f32[16,128,512]{2,0,1:T(8,128)}, f32[16,128,512]{2,0,1:T(8,128)S(1)}, u32[]{:S(2)}, u32[]{:S(2)}) collective-permute-start(f32[16,128,512]{2,0,1:T(8,128)} %copy.194), channel_id=1, source_target_pairs={{0,4},{4,8},{8,12},{12,16},{16,20},{20,24},{24,28},{28,32},{32,36}... | collective-permute-start | bytes 12582920 | tf_op jit(solution)/shard_map/ppermute | solution.py:20
  531.6 95.6 %collective-permute-start.9 = (f32[16,128,512]{2,0,1:T(8,128)}, f32[16,128,512]{2,0,1:T(8,128)}, u32[]{:S(2)}, u32[]{:S(2)}) collective-permute-start(f32[16,128,512]{2,0,1:T(8,128)} %exponential_multiply_fusion.1), channel_id=1, source_target_pairs={{4,0},{8,4},{12,8},{16,12},{20,16},{24,20},{28,24},{32,28},{36,32}... | collective-permute-start | bytes 12582920 | tf_op jit(solution)/shard_map/ppermute | solution.py:21
  533.5 93.7 %collective-permute-start.8 = (f32[16,128,512]{2,0,1:T(8,128)}, f32[16,128,512]{2,0,1:T(8,128)}, u32[]{:S(2)}, u32[]{:S(2)}) collective-permute-start(f32[16,128,512]{2,0,1:T(8,128)} %exponential_multiply_fusion.1), channel_id=1, source_target_pairs={{0,4},{4,8},{8,12},{12,16},{16,20},{20,24},{24,28},{28,32},{32,36}... | collective-permute-start | bytes 12582920 | tf_op jit(solution)/shard_map/ppermute | solution.py:20
  612.6 14.6 %copy-start = (f32[16,128,512]{2,0,1:T(8,128)S(1)}, f32[16,128,512]{2,0,1:T(8,128)}, u32[]{:S(2)}) copy-start(f32[16,128,512]{2,0,1:T(8,128)} %exponential_multiply_fusion.1) | copy-start | bytes 12582916
  621.0 56.2 %collective-permute-start.15 = (f32[1,16,128,512]{3,1,2,0:T(8,128)}, f32[1,16,128,512]{3,1,2,0:T(8,128)}, u32[]{:S(2)}, u32[]{:S(2)}) collective-permute-start(f32[1,16,128,512]{3,1,2,0:T(8,128)} %copy_divide_fusion), channel_id=1, source_target_pairs={{4,0},{8,4},{12,8},{16,12},{20,16},{24,20},{28,24},{32,28},{36,32}... | collective-permute-start | bytes 12582920 | tf_op jit(solution)/shard_map/ppermute | solution.py:21
  622.9 54.3 %collective-permute-start.14 = (f32[1,16,128,512]{3,1,2,0:T(8,128)}, f32[1,16,128,512]{3,1,2,0:T(8,128)}, u32[]{:S(2)}, u32[]{:S(2)}) collective-permute-start(f32[1,16,128,512]{3,1,2,0:T(8,128)} %copy_divide_fusion), channel_id=1, source_target_pairs={{0,4},{4,8},{8,12},{12,16},{16,20},{20,24},{24,28},{28,32},{32,36}... | collective-permute-start | bytes 12582920 | tf_op jit(solution)/shard_map/ppermute | solution.py:20
  671.6 50.7 %collective-permute-start.11 = (f32[1,16,128,512]{3,1,2,0:T(8,128)}, f32[1,16,128,512]{3,1,2,0:T(8,128)}, u32[]{:S(2)}, u32[]{:S(2)}) collective-permute-start(f32[1,16,128,512]{3,1,2,0:T(8,128)} %copy_divide_fusion.2), channel_id=1, source_target_pairs={{4,0},{8,4},{12,8},{16,12},{20,16},{24,20},{28,24},{32,28},{36,32}... | collective-permute-start | bytes 12582920 | tf_op jit(solution)/shard_map/ppermute | solution.py:21
  673.6 58.1 %collective-permute-start.10 = (f32[1,16,128,512]{3,1,2,0:T(8,128)}, f32[1,16,128,512]{3,1,2,0:T(8,128)}, u32[]{:S(2)}, u32[]{:S(2)}) collective-permute-start(f32[1,16,128,512]{3,1,2,0:T(8,128)} %copy_divide_fusion.2), channel_id=1, source_target_pairs={{0,4},{4,8},{8,12},{12,16},{16,20},{20,24},{24,28},{28,32},{32,36}... | collective-permute-start | bytes 12582920 | tf_op jit(solution)/shard_map/ppermute | solution.py:20
  709.5 64.1 %all-to-all-start.3 = ((f32[1,16,128,32,16]{2,4,1,0,3:T(8,128)}), f32[1,16,128,32,16]{2,4,1,0,3:T(8,128)}, u32[]{:S(2)}, u32[]{:S(2)}) async-start(f32[1,16,128,32,16]{2,4,1,0,3:T(8,128)} %fusion.101), calls=%async_computation.3 | async-start | bytes 8388608 | tf_op jit(solution)/shard_map/all_to_all | solution.py:172
  719.0 174.1 %all-reduce.21.cloned.1.call-start = ((), (), s32[]{:S(2)}) async-start(), calls=%async_computation.5 | async-start | bytes 8388608 | tf_op jit(solution)/shard_map/psum | solution.py:176
Sparse Core Ops, SparseCore 0:
  345.4 100.3 all-reduce.18
  789.5 103.5 all-reduce.20
where the time goes:
time: 917 us; the launch traced here: 909 us
  waiting for transfers between devices  309 us (34%)
  matrix products  187 us (20%)
  local copies, waits for them, and re-layouts  145 us (16%)
  blocking collectives  118 us (13%)
  other arithmetic  69.4 us (8%)
  starting transfers between devices  65.8 us (7%)
  between operations  14.1 us (2%)
    psum x2, waiting for transfers between devices, local(): log_total = lax.psum(log_total, 'view')  204 us
    all_to_all x2, blocking collectives, local(): lax.all_to_all(spread, 'owner', split_axis=2, concat_axis=3, tiled=True)  118 us
    ppermute x8, waiting for transfers between devices, extended(): after = lax.ppermute(leading, axis, down)  72.5 us
    dot_general x8, matrix products, along_last(): jnp.einsum('vabns,vsi->vabni', windows, band_matrix(kernel, block_width),...  61.6 us
    reshape x8, local copies, waits for them, and re-layouts, along_last(): volume.reshape(volume.shape[:-1] + (length // block_width, block_width))  42.5 us
    dot_general x4, matrix products, backward(): jnp.einsum('vsyl,vsi->viyl', padded, band_matrix(kernel_first, plane_coun...  35.2 us
    dot_general x4, matrix products, forward(): jnp.einsum('syl,vsi->viyl', padded, band_matrix(kernel_first, plane_count...  34.5 us
    reshape x6, local copies, waits for them, and re-layouts, along_last(): return result.reshape(volume.shape)  33.8 us
  transfers between devices with their start and end apart: 20, of which 12 were waited for; matrix products, arithmetic and copies ran while one was open for 36% of the time, Pallas kernels for 0%

commit v1 on v0

v1 whole, which is shorter than its diff:
```python
import functools

import jax
import jax.numpy as jnp
from jax import lax
from jax.experimental import pallas as pl
from jax.experimental.pallas import tpu as pltpu
from jax.sharding import PartitionSpec as P

ITERS = 2
VA = 4
RIM = 16
BF = jnp.bfloat16
F32 = jnp.float32

COLS = 8
GROUPS = [list(range(8 * g, 8 * g + 8)) for g in range(4)]
Z_UP = [(8 * x + k, 8 * x + 8 + k) for x in range(3) for k in range(8)]
Z_DOWN = [(b, a) for a, b in Z_UP]
X_UP = [(8 * x + k, 8 * x + k + 1) for x in range(4) for k in range(7)]
X_DOWN = [(b, a) for a, b in X_UP]
V_UP = [(i, (i + 1) % 4) for i in range(4)]
V_DOWN = [(b, a) for a, b in V_UP]


def lateral_round(t):
    return [
        (4 * k + r, ((r + t + k // 2) % 4) * 8 + k) for k in range(8) for r in range(4)
    ]


def split(value):
    hi = value.astype(BF)
    lo = (value - hi.astype(F32)).astype(BF)
    return hi, lo


def band(kernel, length, extended):
    rim = RIM if extended else 0
    taps = kernel.shape[-1]
    row = jnp.arange(length)[:, None]
    col = jnp.arange(length + 2 * rim)[None, :]
    offset = col - row + (RIM - rim)
    hit = offset[:, :, None] == jnp.arange(taps)[None, None, :]
    return jnp.sum(jnp.where(hit, kernel[..., None, None, :], 0.0), axis=-1)


def edge_weights(kernel, positions, total):
    source = positions[:, None] + jnp.arange(kernel.shape[-1])[None, :] - RIM
    inside = (source >= 0) & (source < total)
    return jnp.sum(jnp.where(inside, kernel[..., None, :], 0.0), axis=-1)


def split_matrix(value):
    hi = lax.reduce_precision(value, 8, 7)
    return hi.astype(BF), (value - hi).astype(BF)


def left_form(matrix):
    hi, lo = split_matrix(matrix)
    return jnp.concatenate([hi, lo, hi], axis=-1)


def right_form(matrix):
    hi, lo = split_matrix(matrix)
    return jnp.concatenate([hi, lo, hi], axis=-2)


def dot(a, b):
    return lax.dot_general(a, b, (((1,), (0,)), ((), ())), preferred_element_type=F32)


def conv_rows(matrix, data):
    hi, lo = split(data)
    return dot(matrix, jnp.concatenate([hi, hi, lo], axis=0))


def conv_lanes(data, matrix):
    hi, lo = split(data)
    return dot(jnp.concatenate([hi, hi, lo], axis=1), matrix)


def xy_planes(load, mx, my, planes, finish):
    for p in range(0, planes, 2):
        pair = jnp.concatenate([load(p), load(p + 1)], axis=1)
        mid = conv_rows(mx, pair)
        both = jnp.concatenate([mid[:, :128], mid[:, 128:]], axis=0)
        done = conv_lanes(both, my)
        half = done.shape[0] // 2
        finish(p, done[:half])
        finish(p + 1, done[half:])


def forward_kernel(mz_ref, mx_ref, my_ref, f_ref, zb_ref, za_ref, xl_ref, xr_ref, obs_ref, q_ref, w_ref):
    depth, width = f_ref.shape[0], f_ref.shape[1]
    wide = width + 2 * RIM

    @pl.when(pl.program_id(0) == 0)
    def _():
        mz = mz_ref[...]
        w_flat = w_ref.reshape(depth * wide, 128)
        f_flat = f_ref.reshape(depth * width, 128)
        b_flat = zb_ref.reshape(RIM * width, 128)
        a_flat = za_ref.reshape(RIM * width, 128)

        def column(x):
            return jnp.concatenate(
                [
                    b_flat[pl.ds(x, RIM, stride=width), :],
                    f_flat[pl.ds(x, depth, stride=width), :],
                    a_flat[pl.ds(x, RIM, stride=width), :],
                ],
                axis=0,
            )

        def body(i, _):
            x = 2 * i
            out = conv_rows(mz, jnp.concatenate([column(x), column(x + 1)], axis=1))
            w_flat[pl.ds(x + RIM, depth, stride=wide), :] = out[:, :128]
            w_flat[pl.ds(x + 1 + RIM, depth, stride=wide), :] = out[:, 128:]
            return 0

        lax.fori_loop(0, width // 2, body, 0)
        long = depth + 2 * RIM
        for side, base in ((xl_ref, 0), (xr_ref, RIM + width)):
            s_flat = side.reshape(long * RIM, 128)

            def edge(i, _):
                x = 2 * i
                pair = jnp.concatenate(
                    [s_flat[pl.ds(x, long, stride=RIM), :], s_flat[pl.ds(x + 1, long, stride=RIM), :]],
                    axis=1,
                )
                out = conv_rows(mz, pair)
                w_flat[pl.ds(x + base, depth, stride=wide), :] = out[:, :128]
                w_flat[pl.ds(x + 1 + base, depth, stride=wide), :] = out[:, 128:]
                return 0

            lax.fori_loop(0, RIM // 2, edge, 0)

    planes = obs_ref.shape[0]
    first = pl.program_id(0) * planes

    def finish(p, blurred):
        q_ref[p] = obs_ref[p] / blurred

    xy_planes(lambda p: w_ref[first + p], mx_ref[...], my_ref[...], planes, finish)


def back_z_kernel(mz_ref, q_ref, zb_ref, za_ref, r_ref):
    depth, width = q_ref.shape[0], q_ref.shape[1]
    q_flat = q_ref.reshape(depth * width, 128)
    b_flat = zb_ref.reshape(RIM * width, 128)
    a_flat = za_ref.reshape(RIM * width, 128)
    r_flat = r_ref.reshape(depth * width, 128)
    mz = mz_ref[...]

    def column(x):
        return jnp.concatenate(
            [
                b_flat[pl.ds(x, RIM, stride=width), :],
                q_flat[pl.ds(x, depth, stride=width), :],
                a_flat[pl.ds(x, RIM, stride=width), :],
            ],
            axis=0,
        )

    for x in range(0, width, 2):
        out = conv_rows(mz, jnp.concatenate([column(x), column(x + 1)], axis=1))
        r_flat[pl.ds(x, depth, stride=width), :] = out[:, :128]
        r_flat[pl.ds(x + 1, depth, stride=width), :] = out[:, 128:]


def back_xy_kernel(me_ref, w_ref, mx_ref, my_ref, r_ref, xl_ref, xr_ref, *rest):
    acc_ref, l_ref = rest if len(rest) == 2 else (None, rest[0])
    planes = r_ref.shape[0]
    me = me_ref[0]
    weight = w_ref[pl.program_id(0)]

    def load(p):
        return jnp.concatenate([xl_ref[p], r_ref[p], xr_ref[p]], axis=0)

    def finish(p, back):
        term = weight * jnp.log(back)
        for quarter in range(4):
            slot = lax.rem(quarter - me + 4, 4)
            part = term[quarter * 16 : quarter * 16 + 16]
            if acc_ref is not None:
                part = part + acc_ref[slot, p]
            l_ref[slot, p] = part

    xy_planes(load, mx_ref[...], my_ref[...], planes, finish)


def whole(shape):
    return pl.BlockSpec(shape, lambda i: (0,) * len(shape))


def forward(mz, mx, my, f, zb, za, xl, xr, obs):
    depth, width, lines = f.shape
    planes = 16
    moving = pl.BlockSpec((planes, width, lines), lambda i: (i, 0, 0))
    return pl.pallas_call(
        forward_kernel,
        grid=(depth // planes,),
        in_specs=[whole(v.shape) for v in (mz, mx, my, f, zb, za, xl, xr)] + [moving],
        out_specs=moving,
        out_shape=jax.ShapeDtypeStruct(obs.shape, F32),
        scratch_shapes=[pltpu.VMEM((depth, width + 2 * RIM, lines), F32)],
        cost_estimate=pl.CostEstimate(flops=10**10, bytes_accessed=2 * 10**7, transcendentals=0),
        name="forward",
    )(mz, mx, my, f, zb, za, xl, xr, obs)


def back_z(mz, q, zb, za):
    depth, width, lines = q.shape
    group = 8
    part = pl.BlockSpec((depth, group, lines), lambda i: (0, i, 0))
    rim = pl.BlockSpec((RIM, group, lines), lambda i: (0, i, 0))
    return pl.pallas_call(
        back_z_kernel,
        grid=(width // group,),
        in_specs=[whole(mz.shape), part, rim, rim],
        out_specs=part,
        out_shape=jax.ShapeDtypeStruct(q.shape, F32),
        cost_estimate=pl.CostEstimate(flops=3 * 10**9, bytes_accessed=10**7, transcendentals=0),
        name="back_z",
    )(mz, q, zb, za)


def back_xy(me, weight, mx, my, r, xl, xr, acc=None):
    depth, width, lines = r.shape
    planes = 16
    smem = pl.BlockSpec(memory_space=pltpu.SMEM)
    part = pl.BlockSpec((planes, width, lines), lambda i: (i, 0, 0))
    rim = pl.BlockSpec((planes, RIM, lines), lambda i: (i, 0, 0))
    out = pl.BlockSpec((4, planes, width // 4, lines), lambda i: (0, i, 0, 0))
    args = [me, weight, mx, my, r, xl, xr] + ([] if acc is None else [acc])
    return pl.pallas_call(
        back_xy_kernel,
        grid=(depth // planes,),
        in_specs=[smem, smem, whole(mx.shape), whole(my.shape), part, rim, rim]
        + ([] if acc is None else [out]),
        out_specs=out,
        out_shape=jax.ShapeDtypeStruct((4, depth, width // 4, lines), F32),
        cost_estimate=pl.CostEstimate(flops=5 * 10**9, bytes_accessed=10**7, transcendentals=10**6),
        name="back_xy",
    )(*args)


def gather_quarters(quarter, half):
    below = lax.ppermute(quarter, "view", V_UP)
    above = lax.ppermute(quarter, "view", V_DOWN)
    first = lax.ppermute(below[:half], "view", V_UP)
    second = lax.ppermute(above[half:], "view", V_DOWN)
    return quarter, above, jnp.concatenate([first, second], axis=0), below


def scatter_quarters(parts):
    half = parts.shape[1] // 2
    first = lax.ppermute(parts[2, :half], "view", V_UP)
    second = lax.ppermute(parts[2, half:], "view", V_DOWN)
    up = jnp.concatenate([parts[1, :half] + first, parts[1, half:]], axis=0)
    down = jnp.concatenate([parts[3, :half], parts[3, half:] + second], axis=0)
    return parts[0] + lax.ppermute(up, "view", V_UP) + lax.ppermute(down, "view", V_DOWN)


def z_rims(block):
    before = lax.ppermute(block[-RIM:], "owner", Z_UP)
    after = lax.ppermute(block[:RIM], "owner", Z_DOWN)
    return before, after


def x_rims(right_edge, left_edge):
    left = lax.ppermute(right_edge, "owner", X_UP)
    right = lax.ppermute(left_edge, "owner", X_DOWN)
    return left, right


def local(estimate, axial_views, lateral_views, psf_axial, psf_lateral, coverage):
    slab, lines, columns = estimate.shape
    owner = lax.axis_index("owner")
    me = lax.axis_index("view")
    k = owner % 8
    z_chip = owner // 8
    width = columns // COLS
    depth = 8 * slab

    turned = estimate.transpose(0, 2, 1).reshape(slab, COLS, 4, width // 4, lines)
    mine = lax.dynamic_index_in_dim(turned, me, 2, keepdims=False).reshape(slab, -1, lines)
    quarter = lax.all_to_all(
        mine, "owner", split_axis=1, concat_axis=0, axis_index_groups=GROUPS, tiled=True
    )

    axial = lax.all_to_all(
        axial_views[0].transpose(0, 2, 1),
        "owner",
        split_axis=1,
        concat_axis=0,
        axis_index_groups=GROUPS,
        tiled=True,
    )
    chunks = lateral_views[0].transpose(2, 0, 1).reshape(4, depth, slab, lines)
    lateral = jnp.zeros((depth, width, lines), F32)
    for t in range(4):
        target = (owner % 4 + t + z_chip) % 4
        piece = lax.dynamic_index_in_dim(chunks, target, 0, keepdims=False)
        piece = lax.ppermute(piece, "owner", lateral_round(t))
        source = (z_chip - t - k // 2) % 4
        lateral = lax.dynamic_update_slice_in_dim(lateral, piece, source * slab, axis=1)

    cover = jnp.repeat(coverage[0].astype(F32), 2, axis=0)
    cover = lax.all_to_all(
        cover, "owner", split_axis=0, concat_axis=0, axis_index_groups=GROUPS, tiled=True
    )
    count = jnp.sum(cover, axis=-1)
    weight_axial = lax.dynamic_index_in_dim(cover, me, 1, keepdims=False)
    weight_lateral = lax.dynamic_index_in_dim(cover, VA + me, 1, keepdims=False)

    taps = jnp.concatenate([psf_axial, psf_lateral], axis=0)
    taps = taps / jnp.sum(taps, axis=-1, keepdims=True)
    flipped = taps[..., ::-1]
    z_at = z_chip * depth + jnp.arange(depth)
    x_at = k * width + jnp.arange(width)
    y_at = jnp.arange(lines)
    ahead_z = left_form(band(taps[:, 0], depth, True))
    ahead_x = left_form(band(taps[:, 2], width, True))
    ahead_y = right_form(jnp.swapaxes(band(taps[:, 1], lines, False), 1, 2))
    wz = edge_weights(flipped[:, 0], z_at, 4 * depth)
    wx = edge_weights(flipped[:, 2], x_at, columns)
    wy = edge_weights(flipped[:, 1], y_at, lines)
    back_mz = left_form(band(flipped[:, 0], depth, True) / wz[:, :, None])
    back_mx = left_form(band(flipped[:, 2], width, True) / wx[:, :, None])
    back_my = right_form(
        jnp.swapaxes(band(flipped[:, 1], lines, False) / wy[:, :, None], 1, 2)
    )
    me_arr = me[None].astype(jnp.int32)

    for iteration in range(ITERS):
        pieces = gather_quarters(quarter, depth // 2)
        block = jnp.zeros((depth, width, lines), F32)
        for d in range(4):
            at = ((me + d) % 4) * (width // 4)
            block = lax.dynamic_update_slice_in_dim(block, pieces[d], at, axis=1)
        before, after = z_rims(block)
        long_right = jnp.concatenate(
            [before[:, -RIM:], block[:, -RIM:], after[:, -RIM:]], axis=0
        )
        long_left = jnp.concatenate(
            [before[:, :RIM], block[:, :RIM], after[:, :RIM]], axis=0
        )
        left, right = x_rims(long_right, long_left)
        logs = None
        for number, (obs, weight) in enumerate(
            ((axial, weight_axial), (lateral, weight_lateral))
        ):
            quotient = forward(
                ahead_z[number], ahead_x[number], ahead_y[number],
                block, before, after, left, right, obs,
            )
            rz = back_z(back_mz[number], quotient, *z_rims(quotient))
            logs = back_xy(
                me_arr, weight, back_mx[number], back_my[number],
                rz, *x_rims(rz[:, -RIM:], rz[:, :RIM]), acc=logs,
            )
        total = scatter_quarters(logs)
        slabs = total.reshape(8, slab, width // 4, lines) / count[:, None, None, None]
        quarter = quarter * jnp.exp(slabs.reshape(quarter.shape))

    slabs = lax.all_to_all(
        quarter, "owner", split_axis=0, concat_axis=1, axis_index_groups=GROUPS, tiled=True
    )
    slabs = slabs.reshape(slab, COLS, width // 4, lines)
    pieces = gather_quarters(slabs, slab // 2)
    result = jnp.zeros((slab, COLS, 4, width // 4, lines), F32)
    for d in range(4):
        result = lax.dynamic_update_index_in_dim(result, pieces[d], (me + d) % 4, axis=2)
    return result.reshape(slab, columns, lines).transpose(0, 2, 1)


def solution(mesh):
    in_specs = (
        P("owner", None, None),
        P("view", "owner", None, None),
        P("view", "owner", None, None),
        P("view", None, None),
        P("view", None, None),
        P("owner", None, None),
    )
    out_specs = P("owner", None, None)
    return jax.shard_map(local, mesh=mesh, in_specs=in_specs, out_specs=out_specs, check_vma=False)
```

time: 917 us -> 672 us (0.73)
  matrix products: 187 us -> 0 us
  Pallas kernels: 0 us -> 182 us
  waiting for transfers between devices: 309 us -> 198 us
  blocking collectives: 118 us -> 17.5 us
  starting transfers between devices: 65.8 us -> 154 us
  local copies, waits for them, and re-layouts: 145 us -> 88.6 us
  other arithmetic: 69.4 us -> 20.5 us
  between operations: 14.1 us -> 1.21 us
    psum x2 -> x0, waiting for transfers between devices: 204 us -> none  [local(): log_total = lax.psum(log_total, 'view')]
    dot_general x26 -> x0, matrix products: 187 us -> none  [the longest x8 61.6 us: along_last(): jnp.einsum('vabns,vsi->vabni', windows, band_matrix(kernel, block_width),...]
    pallas_call x0 -> x12, Pallas kernels: none -> 182 us  [the longest x4 109 us: forward(): pl.pallas_call(forward_kernel, grid=(depth // planes,), in_specs=[whole(v...]
    ppermute x16 -> x48, waiting for transfers between devices: 93.9 us -> 198 us  [the longest x2 43.4 us: scatter_quarters(): lax.ppermute(down, 'view', V_DOWN)]
    all_to_all x2 -> x1, blocking collectives: 118 us -> 17.5 us  [local(): lax.all_to_all(quarter, 'owner', split_axis=0, concat_axis=1, axis_index_...]
    reshape x18 -> x2, local copies, waits for them, and re-layouts: 98.5 us -> 7.04 us  [the longest x1 5.43 us: local(): chunks = lateral_views[0].transpose(2, 0, 1).reshape(4, depth, slab, lines)]
    ppermute x16 -> x48, starting transfers between devices: 46.7 us -> 125 us  [the longest x6 28.5 us: z_rims(): before = lax.ppermute(block[-RIM:], 'owner', Z_UP)]
    div x6 -> x2, other arithmetic: 33.3 us -> 0.1 us  [the longest x1 0.08 us: local(): taps = taps / jnp.sum(taps, axis=-1, keepdims=True)]
  transfers between devices with their start and end apart: 20 -> 51, of which waited for: 12 -> 23; matrix products, arithmetic and copies ran while one was open for 36% -> 12% of each run, Pallas kernels for 0% -> 20%
where the time goes in v1:
time: 672 us; the launch traced here: 662 us
  waiting for transfers between devices  198 us (29%)
  Pallas kernels  182 us (27%)
  starting transfers between devices  154 us (23%)
  local copies, waits for them, and re-layouts  88.6 us (13%)
  other arithmetic  20.5 us (3%)
  blocking collectives  17.5 us (3%)
    pallas_call x4, Pallas kernels, forward(): pl.pallas_call(forward_kernel, grid=(depth // planes,), in_specs=[whole(v...  109 us
    ppermute x2, waiting for transfers between devices, scatter_quarters(): lax.ppermute(down, 'view', V_DOWN)  43.4 us
    pallas_call x4, Pallas kernels, back_xy(): pl.pallas_call(back_xy_kernel, grid=(depth // planes,), in_specs=[smem, s...  41.1 us
    pallas_call x4, Pallas kernels, back_z(): pl.pallas_call(back_z_kernel, grid=(width // group,), in_specs=[whole(mz....  32 us
    ppermute x3, waiting for transfers between devices, gather_quarters(): above = lax.ppermute(quarter, 'view', V_DOWN)  30.8 us
    ppermute x3, waiting for transfers between devices, gather_quarters(): below = lax.ppermute(quarter, 'view', V_UP)  30 us
    ppermute x6, starting transfers between devices, z_rims(): before = lax.ppermute(block[-RIM:], 'owner', Z_UP)  28.5 us
    ppermute x6, starting transfers between devices, x_rims(): left = lax.ppermute(right_edge, 'owner', X_UP)  22.7 us
  transfers between devices with their start and end apart: 51, of which 23 were waited for; matrix products, arithmetic and copies ran while one was open for 12% of the time, Pallas kernels for 20%

profile of v1, /device:TPU:1, one launch (start us, length us, event | category | flops | bytes accessed | tf_op | source)
XLA Modules:
  0.0 662.0 jit_solution(6112670421092252484)
XLA Ops:
  0.0 5.3 copy.71
  8.3 6.8 %all-to-all-start = ((f32[16,128,128]{2,0,1:T(8,128)}), f32[16,128,128]{2,0,1:T(8,128)S(1)}, u32[]{:S(2)}, u32[]{:S(2)}) async-start(f32[16,128,128]{2,0,1:T(8,128)} %copy.72), calls=%async_computation | async-start | bytes 2097152 | tf_op jit(solution)/shard_map/all_to_all | solution.py:291
  15.1 5.4 copy.99
  20.5 4.0 dynamic-slice_bitcast_fusion
  24.5 4.3 collective-permute-start.10
  28.7 5.6 collective-permute-start.9
  42.8 5.4 copy.90
  50.5 11.0 %all-to-all-start.2 = ((f32[16,512,128]{2,0,1:T(8,128)}), f32[16,512,128]{2,0,1:T(8,128)}, u32[]{:S(2)}, u32[]{:S(2)}) async-start(f32[16,512,128]{2,0,1:T(8,128)} %bitcast.154), calls=%async_computation.2 | async-start | bytes 8388608 | tf_op jit(solution)/shard_map/all_to_all | solution.py:295
  69.7 18.2 %collective-permute-done.1 = f32[128,16,128]{2,1,0:T(8,128)S(1)} collective-permute-done((f32[128,16,128]{2,1,0:T(8,128)S(1)}, f32[128,16,128]{2,1,0:T(8,128)S(1)}, u32[]{:S(2)}, u32[]{:S(2)}) %collective-permute-start.1) | collective-permute-done | bytes 1048608 | tf_op jit(solution)/shard_map/ppermute | solution.py:252
  88.1 2.7 collective-permute-start.3
  92.4 9.4 %collective-permute-done.2 = f32[64,16,128]{2,1,0:T(8,128)S(1)} collective-permute-done((f32[64,16,128]{2,1,0:T(8,128)S(1)}, f32[64,16,128]{2,1,0:T(8,128)S(1)}, u32[]{:S(2)}, u32[]{:S(2)}) %collective-permute-start.2) | collective-permute-done | bytes 524320 | tf_op jit(solution)/shard_map/ppermute | solution.py:254
  104.2 4.0 collective-permute-start.4
  108.4 7.6 %collective-permute-done.5.za_ref = f32[16,64,128]{2,1,0:T(8,128)S(1)} collective-permute-done((f32[16,64,128]{2,1,0:T(8,128)S(1)}, f32[16,64,128]{2,1,0:T(8,128)S(1)}, u32[]{:S(2)}, u32[]{:S(2)}) %collective-permute-start.5) | collective-permute-done | bytes 524320 | tf_op jit(solution)/shard_map/ppermute | solution.py:270
  117.6 5.3 collective-permute-start.6
  142.1 9.6 %collective-permute-done.11 = f32[128,16,128]{2,1,0:T(8,128)} collective-permute-done((f32[128,16,128]{2,1,0:T(8,128)S(1)}, f32[128,16,128]{2,1,0:T(8,128)}, u32[]{:S(2)}, u32[]{:S(2)}) %collective-permute-start.11) | collective-permute-done | bytes 1048608 | tf_op jit(solution)/shard_map/ppermute | solution.py:308
  154.7 11.1 %all-to-all-start.1 = ((f32[8,1,8]{2,1,0:T(1,128)}), f32[8,1,8]{2,1,0:T(1,128)S(1)}, u32[]{:S(2)}, u32[]{:S(2)}) async-start(f32[8,1,8]{2,1,0:T(1,128)} %bitcast.10), calls=%async_computation.1 | async-start | bytes 8192 | tf_op jit(solution)/shard_map/all_to_all | solution.py:313
  165.8 5.4 copy.92
  171.2 27.1 %forward.5.q_ref = f32[128,64,128]{2,1,0:T(8,128)} custom-call(bf16[128,480]{1,0:T(8,128)(2,1)} %get-tuple-element.61.mz_ref, bf16[64,288]{1,0:T(8,128)(2,1)} %get-tuple-element.77.mx_ref, bf16[384,128]{1,0:T(8,128)(2,1)} %get-tuple-element.69.my_ref, f32[128,64,128]{2,1,0:T(8,128)} %copy-done.1, f32[16,64,128]{2,1,0:T(8,128)} %copy-done.8, ...), custom_call_target="tpu_custom_call" | custom-call | flops 10000000000 | bytes 20000000 | tf_op jit(solution)/shard_map/forward/pallas_call | solution.py:203
  200.9 6.1 collective-permute-start.16
  207.0 27.2 %forward.4.q_ref = f32[128,64,128]{2,1,0:T(8,128)} custom-call(bf16[128,480]{1,0:T(8,128)(2,1)} %get-tuple-element.62.mz_ref, bf16[64,288]{1,0:T(8,128)(2,1)} %get-tuple-element.78.mx_ref, bf16[384,128]{1,0:T(8,128)(2,1)} %get-tuple-element.70.my_ref, f32[128,64,128]{2,1,0:T(8,128)} %copy-done.1, f32[16,64,128]{2,1,0:T(8,128)} %copy-done.8, ...), custom_call_target="tpu_custom_call" | custom-call | flops 10000000000 | bytes 20000000 | tf_op jit(solution)/shard_map/forward/pallas_call | solution.py:203
  237.7 4.8 collective-permute-start.12
  243.6 8.1 %back_z.5.r_ref = f32[128,64,128]{2,1,0:T(8,128)} custom-call(bf16[128,480]{1,0:T(8,128)(2,1)} %get-tuple-element.63.mz_ref, f32[128,64,128]{2,1,0:T(8,128)} %forward.5.q_ref, f32[16,64,128]{2,1,0:T(8,128)} %copy-done.20, f32[16,64,128]{2,1,0:T(8,128)} %copy-done.18), custom_call_target="tpu_custom_call" | custom-call | flops 3000000000 | bytes 10000000 | tf_op jit(solution)/shard_map/back_z/pallas_call | solution.py:220
  253.3 2.8 collective-permute-start.19
  256.1 3.5 collective-permute-start.18
  259.7 8.0 %back_z.4.r_ref = f32[128,64,128]{2,1,0:T(8,128)} custom-call(bf16[128,480]{1,0:T(8,128)(2,1)} %get-tuple-element.64.mz_ref, f32[128,64,128]{2,1,0:T(8,128)} %forward.4.q_ref, f32[16,64,128]{2,1,0:T(8,128)} %collective-permute-done.12.zb_ref, f32[16,64,128]{2,1,0:T(8,128)} %collective-permute-done.13.za_ref), custom_call_target="tpu_custom_call" | custom-call | flops 3000000000 | bytes 10000000 | tf_op jit(solution)/shard_map/back_z/pallas_call | solution.py:220
  267.7 3.1 fusion.40
  272.7 3.6 collective-permute-start.14
  278.6 9.9 %back_xy.4.rest_0_ = f32[4,128,16,128]{3,2,1,0:T(8,128)} custom-call(s32[1]{0:T(128)} %bitcast.7.me_ref, f32[8]{0:T(128)} %get-tuple-element.11.w_ref, bf16[64,288]{1,0:T(8,128)(2,1)} %get-tuple-element.79.mx_ref, bf16[384,128]{1,0:T(8,128)(2,1)} %get-tuple-element.71.my_ref, f32[128,64,128]{2,1,0:T(8,128)} %back_z.5.r_ref, ...), custom_call_target="tpu_custom_call" | custom-call | flops 5000000000 | bytes 10000000 | tf_op jit(solution)/shard_map/back_xy/pallas_call | solution.py:239
  288.5 10.7 %back_xy.5 = f32[4,128,16,128]{3,2,1,0:T(8,128)} custom-call(s32[1]{0:T(128)} %bitcast.7.me_ref, f32[8]{0:T(128)} %get-tuple-element.12.w_ref, bf16[64,288]{1,0:T(8,128)(2,1)} %get-tuple-element.80.mx_ref, bf16[384,128]{1,0:T(8,128)(2,1)} %get-tuple-element.72.my_ref, f32[128,64,128]{2,1,0:T(8,128)} %back_z.4.r_ref, ...), custom_call_target="tpu_custom_call" | custom-call | flops 5000000000 | bytes 10000000 | tf_op jit(solution)/shard_map/back_xy/pallas_call | solution.py:239
  303.6 12.3 %collective-permute-done.20 = f32[64,16,128]{2,1,0:T(8,128)S(1)} collective-permute-done((f32[64,16,128]{2,1,0:T(8,128)S(1)}, f32[64,16,128]{2,1,0:T(8,128)S(1)}, u32[]{:S(2)}, u32[]{:S(2)}) %collective-permute-start.20) | collective-permute-done | bytes 524320 | tf_op jit(solution)/shard_map/ppermute | solution.py:261
  320.2 21.4 %collective-permute-done.23 = f32[128,16,128]{2,1,0:T(8,128)} collective-permute-done((f32[128,16,128]{2,1,0:T(8,128)S(1)}, f32[128,16,128]{2,1,0:T(8,128)}, u32[]{:S(2)}, u32[]{:S(2)}) %collective-permute-start.23) | collective-permute-done | bytes 1048608 | tf_op jit(solution)/shard_map/ppermute | solution.py:265
  341.6 3.2 collective-permute-done.21
  347.6 12.1 %collective-permute-start.24 = (f32[128,16,128]{2,1,0:T(8,128)S(1)}, f32[128,16,128]{2,1,0:T(8,128)S(1)}, u32[]{:S(2)}, u32[]{:S(2)}) collective-permute-start(f32[128,16,128]{2,1,0:T(8,128)S(1)} %get-tuple-element.92), channel_id=1, source_target_pairs={{1,0},{2,1},{3,2},{0,3},{5,4},{6,5},{7,6},{4,7},{9,8},{10,9},{11,1... | collective-permute-start | bytes 3145736 | tf_op jit(solution)/shard_map/ppermute | solution.py:253
  359.6 11.9 %collective-permute-done.25 = f32[128,16,128]{2,1,0:T(8,128)S(1)} collective-permute-done((f32[128,16,128]{2,1,0:T(8,128)S(1)}, f32[128,16,128]{2,1,0:T(8,128)S(1)}, u32[]{:S(2)}, u32[]{:S(2)}) %collective-permute-start.25) | collective-permute-done | bytes 1048608 | tf_op jit(solution)/shard_map/ppermute | solution.py:252
  371.6 8.4 %collective-permute-done.24 = f32[128,16,128]{2,1,0:T(8,128)S(1)} collective-permute-done((f32[128,16,128]{2,1,0:T(8,128)S(1)}, f32[128,16,128]{2,1,0:T(8,128)S(1)}, u32[]{:S(2)}, u32[]{:S(2)}) %collective-permute-start.24) | collective-permute-done | bytes 1048608 | tf_op jit(solution)/shard_map/ppermute | solution.py:253
  380.0 3.3 collective-permute-start.27
  383.5 8.0 %collective-permute-done.27 = f32[64,16,128]{2,1,0:T(8,128)S(1)} collective-permute-done((f32[64,16,128]{2,1,0:T(8,128)S(1)}, f32[64,16,128]{2,1,0:T(8,128)S(1)}, u32[]{:S(2)}, u32[]{:S(2)}) %collective-permute-start.27) | collective-permute-done | bytes 524320 | tf_op jit(solution)/shard_map/ppermute | solution.py:255
  393.2 4.0 collective-permute-start.28
  397.4 5.9 collective-permute-done.29.za_ref
  404.3 2.9 collective-permute-start.30
  407.3 5.5 collective-permute-start.31
  412.8 8.9 %collective-permute-done.30.xl_ref = f32[160,16,128]{2,1,0:T(8,128)S(1)} collective-permute-done((f32[160,16,128]{2,1,0:T(8,128)S(1)}, f32[160,16,128]{2,1,0:T(8,128)S(1)}, u32[]{:S(2)}, u32[]{:S(2)}) %collective-permute-start.30) | collective-permute-done | bytes 1310752 | tf_op jit(solution)/shard_map/ppermute | solution.py:275
  422.8 3.5 collective-permute-done.31.xr_ref
  426.3 27.2 %forward.7.q_ref = f32[128,64,128]{2,1,0:T(8,128)} custom-call(bf16[128,480]{1,0:T(8,128)(2,1)} %get-tuple-element.61.mz_ref, bf16[64,288]{1,0:T(8,128)(2,1)} %get-tuple-element.77.mx_ref, bf16[384,128]{1,0:T(8,128)(2,1)} %get-tuple-element.69.my_ref, f32[128,64,128]{2,1,0:T(8,128)} %copy-done, f32[16,64,128]{2,1,0:T(8,128)} %copy-done.10, ...), custom_call_target="tpu_custom_call" | custom-call | flops 10000000000 | bytes 20000000 | tf_op jit(solution)/shard_map/forward/pallas_call | solution.py:203
  456.1 4.8 collective-permute-start.36
  460.9 27.1 %forward.6.q_ref = f32[128,64,128]{2,1,0:T(8,128)} custom-call(bf16[128,480]{1,0:T(8,128)(2,1)} %get-tuple-element.62.mz_ref, bf16[64,288]{1,0:T(8,128)(2,1)} %get-tuple-element.78.mx_ref, bf16[384,128]{1,0:T(8,128)(2,1)} %get-tuple-element.70.my_ref, f32[128,64,128]{2,1,0:T(8,128)} %copy-done, f32[16,64,128]{2,1,0:T(8,128)} %copy-done.10, ...), custom_call_target="tpu_custom_call" | custom-call | flops 10000000000 | bytes 20000000 | tf_op jit(solution)/shard_map/forward/pallas_call | solution.py:203
  491.5 4.8 collective-permute-start.32
  498.0 8.0 %back_z.7.r_ref = f32[128,64,128]{2,1,0:T(8,128)} custom-call(bf16[128,480]{1,0:T(8,128)(2,1)} %get-tuple-element.63.mz_ref, f32[128,64,128]{2,1,0:T(8,128)} %forward.7.q_ref, f32[16,64,128]{2,1,0:T(8,128)} %copy-done.19, f32[16,64,128]{2,1,0:T(8,128)} %copy-done.17), custom_call_target="tpu_custom_call" | custom-call | flops 3000000000 | bytes 10000000 | tf_op jit(solution)/shard_map/back_z/pallas_call | solution.py:220
  509.6 3.6 collective-permute-start.38
  513.3 8.0 %back_z.6.r_ref = f32[128,64,128]{2,1,0:T(8,128)} custom-call(bf16[128,480]{1,0:T(8,128)(2,1)} %get-tuple-element.64.mz_ref, f32[128,64,128]{2,1,0:T(8,128)} %forward.6.q_ref, f32[16,64,128]{2,1,0:T(8,128)} %collective-permute-done.32.zb_ref, f32[16,64,128]{2,1,0:T(8,128)} %collective-permute-done.33.za_ref), custom_call_target="tpu_custom_call" | custom-call | flops 3000000000 | bytes 10000000 | tf_op jit(solution)/shard_map/back_z/pallas_call | solution.py:220
  521.3 3.1 fusion.34
  526.3 3.6 collective-permute-start.34
  530.0 9.9 %back_xy.6.rest_0_ = f32[4,128,16,128]{3,2,1,0:T(8,128)} custom-call(s32[1]{0:T(128)} %bitcast.7.me_ref, f32[8]{0:T(128)} %get-tuple-element.11.w_ref, bf16[64,288]{1,0:T(8,128)(2,1)} %get-tuple-element.79.mx_ref, bf16[384,128]{1,0:T(8,128)(2,1)} %get-tuple-element.71.my_ref, f32[128,64,128]{2,1,0:T(8,128)} %back_z.7.r_ref, ...), custom_call_target="tpu_custom_call" | custom-call | flops 5000000000 | bytes 10000000 | tf_op jit(solution)/shard_map/back_xy/pallas_call | solution.py:239
  542.0 10.7 %back_xy.7 = f32[4,128,16,128]{3,2,1,0:T(8,128)} custom-call(s32[1]{0:T(128)} %bitcast.7.me_ref, f32[8]{0:T(128)} %get-tuple-element.12.w_ref, bf16[64,288]{1,0:T(8,128)(2,1)} %get-tuple-element.80.mx_ref, bf16[384,128]{1,0:T(8,128)(2,1)} %get-tuple-element.72.my_ref, f32[128,64,128]{2,1,0:T(8,128)} %back_z.6.r_ref, ...), custom_call_target="tpu_custom_call" | custom-call | flops 5000000000 | bytes 10000000 | tf_op jit(solution)/shard_map/back_xy/pallas_call | solution.py:239
  554.5 3.5 collective-permute-start.42
  558.0 9.9 %collective-permute-done.40 = f32[64,16,128]{2,1,0:T(8,128)S(1)} collective-permute-done((f32[64,16,128]{2,1,0:T(8,128)S(1)}, f32[64,16,128]{2,1,0:T(8,128)S(1)}, u32[]{:S(2)}, u32[]{:S(2)}) %collective-permute-start.40) | collective-permute-done | bytes 524320 | tf_op jit(solution)/shard_map/ppermute | solution.py:261
  568.2 3.1 collective-permute-start.43
  571.4 22.0 %collective-permute-done.43 = f32[128,16,128]{2,1,0:T(8,128)S(1)} collective-permute-done((f32[128,16,128]{2,1,0:T(8,128)S(1)}, f32[128,16,128]{2,1,0:T(8,128)S(1)}, u32[]{:S(2)}, u32[]{:S(2)}) %collective-permute-start.43) | collective-permute-done | bytes 1048608 | tf_op jit(solution)/shard_map/ppermute | solution.py:265
  593.5 3.5 collective-permute-done.41
  597.4 17.5 %all_to_all.60 = f32[128,16,128]{2,1,0:T(8,128)S(1)} all-to-all(f32[128,16,128]{2,1,0:T(8,128)S(1)} %fusion.4), channel_id=1, replica_groups={{0,4,8,12,16,20,24,28},{32,36,40,44,48,52,56,60},{64,68,72,76,80,84,88,..., dimensions={0} | all-to-all | bytes 2097152 | tf_op jit(solution)/shard_map/all_to_all | solution.py:370
  617.5 22.4 %collective-permute-done.44 = f32[16,8,16,128]{3,2,1,0:T(8,128)S(1)} collective-permute-done((f32[16,8,16,128]{3,2,1,0:T(8,128)}, f32[16,8,16,128]{3,2,1,0:T(8,128)S(1)}, u32[]{:S(2)}, u32[]{:S(2)}) %collective-permute-start.44) | collective-permute-done | bytes 1048608 | tf_op jit(solution)/shard_map/ppermute | solution.py:253
  646.4 5.2 collective-permute-done.47
  651.6 2.6 collective-permute-done.46
  656.5 5.3 copy.97
  (214 shorter events, 107.6 us)
Async XLA Ops:
  8.3 42.2 %all-to-all-start = ((f32[16,128,128]{2,0,1:T(8,128)}), f32[16,128,128]{2,0,1:T(8,128)S(1)}, u32[]{:S(2)}, u32[]{:S(2)}) async-start(f32[16,128,128]{2,0,1:T(8,128)} %copy.72), calls=%async_computation | async-start | bytes 2097152 | tf_op jit(solution)/shard_map/all_to_all | solution.py:291
  20.5 15.9 %copy-start.13 = (f32[1,3,33]{2,0,1:T(1,128)S(1)}, f32[1,3,33]{2,0,1:T(1,128)}, u32[]{:S(2)}) copy-start(f32[1,3,33]{2,0,1:T(1,128)} %param.10) | copy-start | bytes 1192
  20.5 15.9 %copy-start.14 = (f32[1,3,33]{2,0,1:T(1,128)S(1)}, f32[1,3,33]{2,0,1:T(1,128)}, u32[]{:S(2)}) copy-start(f32[1,3,33]{2,0,1:T(1,128)} %param.9) | copy-start | bytes 1192
  24.5 115.4 %collective-permute-start.10 = (f32[128,16,128]{2,1,0:T(8,128)}, f32[128,16,128]{2,1,0:T(8,128)}, u32[]{:S(2)}, u32[]{:S(2)}) collective-permute-start(f32[128,16,128]{2,1,0:T(8,128)} %get-tuple-element.46), channel_id=1, source_target_pairs={{0,64},{4,96},{8,0},{12,32},{16,68},{20,100},{24,4},{28,36},{32,10... | collective-permute-start | bytes 3145736 | tf_op jit(solution)/shard_map/ppermute | solution.py:308
  28.7 108.8 %collective-permute-start.9 = (f32[128,16,128]{2,1,0:T(8,128)}, f32[128,16,128]{2,1,0:T(8,128)}, u32[]{:S(2)}, u32[]{:S(2)}) collective-permute-start(f32[128,16,128]{2,1,0:T(8,128)} %get-tuple-element.47), channel_id=1, source_target_pairs={{0,32},{4,64},{8,96},{12,0},{16,36},{20,68},{24,100},{28,4},{32,72... | collective-permute-start | bytes 3145736 | tf_op jit(solution)/shard_map/ppermute | solution.py:308
  34.4 91.6 %collective-permute-start.8 = (f32[128,16,128]{2,1,0:T(8,128)}, f32[128,16,128]{2,1,0:T(8,128)}, u32[]{:S(2)}, u32[]{:S(2)}) collective-permute-start(f32[128,16,128]{2,1,0:T(8,128)} %get-tuple-element.48), channel_id=1, source_target_pairs={{0,0},{4,32},{8,64},{12,96},{16,4},{20,36},{24,68},{28,100},{32,40... | collective-permute-start | bytes 3145736 | tf_op jit(solution)/shard_map/ppermute | solution.py:308
  50.5 103.6 %all-to-all-start.2 = ((f32[16,512,128]{2,0,1:T(8,128)}), f32[16,512,128]{2,0,1:T(8,128)}, u32[]{:S(2)}, u32[]{:S(2)}) async-start(f32[16,512,128]{2,0,1:T(8,128)} %bitcast.154), calls=%async_computation.2 | async-start | bytes 8388608 | tf_op jit(solution)/shard_map/all_to_all | solution.py:295
  61.5 29.3 %copy-start.5 = (f32[2,64,96]{2,1,0:T(8,128)S(1)}, f32[2,64,96]{2,1,0:T(8,128)}, u32[]{:S(2)}) copy-start(f32[2,64,96]{2,1,0:T(8,128)} %get-tuple-element.9) | copy-start | bytes 147460
  61.5 29.3 %copy-start.6 = (f32[2,64,96]{2,1,0:T(8,128)S(1)}, f32[2,64,96]{2,1,0:T(8,128)}, u32[]{:S(2)}) copy-start(f32[2,64,96]{2,1,0:T(8,128)} %get-tuple-element.10) | copy-start | bytes 147460
  61.8 26.1 %collective-permute-start.1 = (f32[128,16,128]{2,1,0:T(8,128)S(1)}, f32[128,16,128]{2,1,0:T(8,128)S(1)}, u32[]{:S(2)}, u32[]{:S(2)}) collective-permute-start(f32[128,16,128]{2,1,0:T(8,128)S(1)} %bitcast.157), channel_id=1, source_target_pairs={{0,1},{1,2},{2,3},{3,0},{4,5},{5,6},{6,7},{7,4},{8,9},{9,10},{10,1... | collective-permute-start | bytes 3145736 | tf_op jit(solution)/shard_map/ppermute | solution.py:252
  63.2 24.8 %collective-permute-start = (f32[128,16,128]{2,1,0:T(8,128)S(1)}, f32[128,16,128]{2,1,0:T(8,128)S(1)}, u32[]{:S(2)}, u32[]{:S(2)}) collective-permute-start(f32[128,16,128]{2,1,0:T(8,128)S(1)} %bitcast.158), channel_id=1, source_target_pairs={{1,0},{2,1},{3,2},{0,3},{5,4},{6,5},{7,6},{4,7},{9,8},{10,9},{11,1... | collective-permute-start | bytes 3145736 | tf_op jit(solution)/shard_map/ppermute | solution.py:253
  87.9 13.9 %collective-permute-start.2 = (f32[64,16,128]{2,1,0:T(8,128)S(1)}, f32[64,16,128]{2,1,0:T(8,128)S(1)}, u32[]{:S(2)}, u32[]{:S(2)}) collective-permute-start(f32[64,16,128]{2,1,0:T(8,128)S(1)} %slice.307), channel_id=1, source_target_pairs={{0,1},{1,2},{2,3},{3,0},{4,5},{5,6},{6,7},{7,4},{8,9},{9,10},{10,1... | collective-permute-start | bytes 1572872 | tf_op jit(solution)/shard_map/ppermute | solution.py:254
  88.1 13.8 %collective-permute-start.3 = (f32[64,16,128]{2,1,0:T(8,128)S(1)}, f32[64,16,128]{2,1,0:T(8,128)S(1)}, u32[]{:S(2)}, u32[]{:S(2)}) collective-permute-start(f32[64,16,128]{2,1,0:T(8,128)S(1)} %slice.308), channel_id=1, source_target_pairs={{1,0},{2,1},{3,2},{0,3},{5,4},{6,5},{7,6},{4,7},{9,8},{10,9},{11,1... | collective-permute-start | bytes 1572872 | tf_op jit(solution)/shard_map/ppermute | solution.py:255
  102.1 15.5 %copy-start.1 = (f32[128,64,128]{2,1,0:T(8,128)}, f32[128,64,128]{2,1,0:T(8,128)S(1)}, u32[]{:S(2)}) copy-start(f32[128,64,128]{2,1,0:T(8,128)S(1)} %constant_dynamic-update-slice_fusion.7.f_ref) | copy-start | bytes 12582916
  102.3 13.8 %collective-permute-start.5 = (f32[16,64,128]{2,1,0:T(8,128)S(1)}, f32[16,64,128]{2,1,0:T(8,128)S(1)}, u32[]{:S(2)}, u32[]{:S(2)}) collective-permute-start(f32[16,64,128]{2,1,0:T(8,128)S(1)} %get-tuple-element.51), channel_id=1, source_target_pairs={{32,0},{36,4},{40,8},{44,12},{48,16},{52,20},{56,24},{60,28},{64,3... | collective-permute-start | bytes 1572872 | tf_op jit(solution)/shard_map/ppermute | solution.py:270
  104.2 13.3 %collective-permute-start.4 = (f32[16,64,128]{2,1,0:T(8,128)S(1)}, f32[16,64,128]{2,1,0:T(8,128)S(1)}, u32[]{:S(2)}, u32[]{:S(2)}) collective-permute-start(f32[16,64,128]{2,1,0:T(8,128)S(1)} %get-tuple-element.52), channel_id=1, source_target_pairs={{0,32},{4,36},{8,40},{12,44},{16,48},{20,52},{24,56},{28,60},{32,6... | collective-permute-start | bytes 1572872 | tf_op jit(solution)/shard_map/ppermute | solution.py:269
  108.4 17.6 %copy-start.15 = (s32[1,4,8]{2,1,0:T(4,128)S(1)}, s32[1,4,8]{2,1,0:T(4,128)}, u32[]{:S(2)}) copy-start(s32[1,4,8]{2,1,0:T(4,128)} %param.11) | copy-start | bytes 388
  116.0 12.2 %copy-start.7 = (f32[16,64,128]{2,1,0:T(8,128)}, f32[16,64,128]{2,1,0:T(8,128)S(1)}, u32[]{:S(2)}) copy-start(f32[16,64,128]{2,1,0:T(8,128)S(1)} %collective-permute-done.5.za_ref) | copy-start | bytes 1572868
  117.5 10.8 %copy-start.8 = (f32[16,64,128]{2,1,0:T(8,128)}, f32[16,64,128]{2,1,0:T(8,128)S(1)}, u32[]{:S(2)}) copy-start(f32[16,64,128]{2,1,0:T(8,128)S(1)} %collective-permute-done.4.zb_ref) | copy-start | bytes 1572868
  117.6 53.6 %collective-permute-start.6 = (f32[160,16,128]{2,1,0:T(8,128)S(1)}, f32[160,16,128]{2,1,0:T(8,128)}, u32[]{:S(2)}, u32[]{:S(2)}) collective-permute-start(f32[160,16,128]{2,1,0:T(8,128)S(1)} %pad_maximum_fusion), channel_id=1, source_target_pairs={{0,4},{4,8},{8,12},{12,16},{16,20},{20,24},{24,28},{32,36},{36,40}... | collective-permute-start | bytes 3932168 | tf_op jit(solution)/shard_map/ppermute | solution.py:275
  124.1 47.1 %collective-permute-start.7 = (f32[160,16,128]{2,1,0:T(8,128)}, f32[160,16,128]{2,1,0:T(8,128)}, u32[]{:S(2)}, u32[]{:S(2)}) collective-permute-start(f32[160,16,128]{2,1,0:T(8,128)} %pad_maximum_fusion.1), channel_id=1, source_target_pairs={{4,0},{8,4},{12,8},{16,12},{20,16},{24,20},{28,24},{36,32},{40,36}... | collective-permute-start | bytes 3932168 | tf_op jit(solution)/shard_map/ppermute | solution.py:276
  126.0 25.7 %collective-permute-start.11 = (f32[128,16,128]{2,1,0:T(8,128)S(1)}, f32[128,16,128]{2,1,0:T(8,128)}, u32[]{:S(2)}, u32[]{:S(2)}) collective-permute-start(f32[128,16,128]{2,1,0:T(8,128)S(1)} %get-tuple-element.45), channel_id=1, source_target_pairs={{0,96},{4,0},{8,32},{12,64},{16,100},{20,4},{24,36},{28,68},{32,8}... | collective-permute-start | bytes 3145736 | tf_op jit(solution)/shard_map/ppermute | solution.py:308
  154.7 123.1 %all-to-all-start.1 = ((f32[8,1,8]{2,1,0:T(1,128)}), f32[8,1,8]{2,1,0:T(1,128)S(1)}, u32[]{:S(2)}, u32[]{:S(2)}) async-start(f32[8,1,8]{2,1,0:T(1,128)} %bitcast.10), calls=%async_computation.1 | async-start | bytes 8192 | tf_op jit(solution)/shard_map/all_to_all | solution.py:313
  199.6 43.0 %collective-permute-start.17 = (f32[16,64,128]{2,1,0:T(8,128)S(1)}, f32[16,64,128]{2,1,0:T(8,128)S(1)}, u32[]{:S(2)}, u32[]{:S(2)}) collective-permute-start(f32[16,64,128]{2,1,0:T(8,128)S(1)} %get-tuple-element.39), channel_id=1, source_target_pairs={{32,0},{36,4},{40,8},{44,12},{48,16},{52,20},{56,24},{60,28},{64,3... | collective-permute-start | bytes 1572872 | tf_op jit(solution)/shard_map/ppermute | solution.py:270
  200.9 41.7 %collective-permute-start.16 = (f32[16,64,128]{2,1,0:T(8,128)S(1)}, f32[16,64,128]{2,1,0:T(8,128)S(1)}, u32[]{:S(2)}, u32[]{:S(2)}) collective-permute-start(f32[16,64,128]{2,1,0:T(8,128)S(1)} %get-tuple-element.40), channel_id=1, source_target_pairs={{0,32},{4,36},{8,40},{12,44},{16,48},{20,52},{24,56},{28,60},{32,6... | collective-permute-start | bytes 1572872 | tf_op jit(solution)/shard_map/ppermute | solution.py:269
  236.4 23.2 %collective-permute-start.13 = (f32[16,64,128]{2,1,0:T(8,128)}, f32[16,64,128]{2,1,0:T(8,128)}, u32[]{:S(2)}, u32[]{:S(2)}) collective-permute-start(f32[16,64,128]{2,1,0:T(8,128)} %get-tuple-element.43), channel_id=1, source_target_pairs={{32,0},{36,4},{40,8},{44,12},{48,16},{52,20},{56,24},{60,28},{64,3... | collective-permute-start | bytes 1572872 | tf_op jit(solution)/shard_map/ppermute | solution.py:270
  237.7 21.9 %collective-permute-start.12 = (f32[16,64,128]{2,1,0:T(8,128)}, f32[16,64,128]{2,1,0:T(8,128)}, u32[]{:S(2)}, u32[]{:S(2)}) collective-permute-start(f32[16,64,128]{2,1,0:T(8,128)} %get-tuple-element.44), channel_id=1, source_target_pairs={{0,32},{4,36},{8,40},{12,44},{16,48},{20,52},{24,56},{28,60},{32,6... | collective-permute-start | bytes 1572872 | tf_op jit(solution)/shard_map/ppermute | solution.py:269
  253.3 25.3 %collective-permute-start.19 = (f32[128,16,128]{2,1,0:T(8,128)S(1)}, f32[128,16,128]{2,1,0:T(8,128)}, u32[]{:S(2)}, u32[]{:S(2)}) collective-permute-start(f32[128,16,128]{2,1,0:T(8,128)S(1)} %get-tuple-element.37), channel_id=1, source_target_pairs={{4,0},{8,4},{12,8},{16,12},{20,16},{24,20},{28,24},{36,32},{40,36}... | collective-permute-start | bytes 3145736 | tf_op jit(solution)/shard_map/ppermute | solution.py:276
  256.1 22.5 %collective-permute-start.18 = (f32[128,16,128]{2,1,0:T(8,128)S(1)}, f32[128,16,128]{2,1,0:T(8,128)}, u32[]{:S(2)}, u32[]{:S(2)}) collective-permute-start(f32[128,16,128]{2,1,0:T(8,128)S(1)} %get-tuple-element.38), channel_id=1, source_target_pairs={{0,4},{4,8},{8,12},{12,16},{16,20},{20,24},{24,28},{32,36},{36,40}... | collective-permute-start | bytes 3145736 | tf_op jit(solution)/shard_map/ppermute | solution.py:275
  267.6 8.8 %copy-start.4 = (bf16[2,128,128]{2,1,0:T(8,128)(2,1)S(1)}, bf16[2,128,128]{2,1,0:T(8,128)(2,1)}, u32[]{:S(2)}) copy-start(bf16[2,128,128]{2,1,0:T(8,128)(2,1)} %get-tuple-element.74) | copy-start | bytes 196612
  270.7 17.7 %collective-permute-start.15 = (f32[128,16,128]{2,1,0:T(8,128)}, f32[128,16,128]{2,1,0:T(8,128)}, u32[]{:S(2)}, u32[]{:S(2)}) collective-permute-start(f32[128,16,128]{2,1,0:T(8,128)} %get-tuple-element.41), channel_id=1, source_target_pairs={{4,0},{8,4},{12,8},{16,12},{20,16},{24,20},{28,24},{36,32},{40,36}... | collective-permute-start | bytes 3145736 | tf_op jit(solution)/shard_map/ppermute | solution.py:276
  272.7 15.8 %collective-permute-start.14 = (f32[128,16,128]{2,1,0:T(8,128)}, f32[128,16,128]{2,1,0:T(8,128)}, u32[]{:S(2)}, u32[]{:S(2)}) collective-permute-start(f32[128,16,128]{2,1,0:T(8,128)} %get-tuple-element.42), channel_id=1, source_target_pairs={{0,4},{4,8},{8,12},{12,16},{16,20},{20,24},{24,28},{32,36},{36,40}... | collective-permute-start | bytes 3145736 | tf_op jit(solution)/shard_map/ppermute | solution.py:275
  300.8 15.0 %collective-permute-start.20 = (f32[64,16,128]{2,1,0:T(8,128)S(1)}, f32[64,16,128]{2,1,0:T(8,128)S(1)}, u32[]{:S(2)}, u32[]{:S(2)}) collective-permute-start(f32[64,16,128]{2,1,0:T(8,128)S(1)} %get-tuple-element.33), channel_id=1, source_target_pairs={{0,1},{1,2},{2,3},{3,0},{4,5},{5,6},{6,7},{7,4},{8,9},{9,10},{10,1... | collective-permute-start | bytes 1572872 | tf_op jit(solution)/shard_map/ppermute | solution.py:261
  301.0 14.8 %collective-permute-start.22 = (f32[64,16,128]{2,1,0:T(8,128)S(1)}, f32[64,16,128]{2,1,0:T(8,128)S(1)}, u32[]{:S(2)}, u32[]{:S(2)}) collective-permute-start(f32[64,16,128]{2,1,0:T(8,128)S(1)} %get-tuple-element.34), channel_id=1, source_target_pairs={{1,0},{2,1},{3,2},{0,3},{5,4},{6,5},{7,6},{4,7},{9,8},{10,9},{11,1... | collective-permute-start | bytes 1572872 | tf_op jit(solution)/shard_map/ppermute | solution.py:262
  317.3 24.3 %collective-permute-start.23 = (f32[128,16,128]{2,1,0:T(8,128)S(1)}, f32[128,16,128]{2,1,0:T(8,128)}, u32[]{:S(2)}, u32[]{:S(2)}) collective-permute-start(f32[128,16,128]{2,1,0:T(8,128)S(1)} %pad_maximum_fusion.5), channel_id=1, source_target_pairs={{1,0},{2,1},{3,2},{0,3},{5,4},{6,5},{7,6},{4,7},{9,8},{10,9},{11,1... | collective-permute-start | bytes 3145736 | tf_op jit(solution)/shard_map/ppermute | solution.py:265
  319.8 25.0 %collective-permute-start.21 = (f32[128,16,128]{2,1,0:T(8,128)S(1)}, f32[128,16,128]{2,1,0:T(8,128)}, u32[]{:S(2)}, u32[]{:S(2)}) collective-permute-start(f32[128,16,128]{2,1,0:T(8,128)S(1)} %pad_maximum_fusion.4), channel_id=1, source_target_pairs={{0,1},{1,2},{2,3},{3,0},{4,5},{5,6},{6,7},{7,4},{8,9},{9,10},{10,1... | collective-permute-start | bytes 3145736 | tf_op jit(solution)/shard_map/ppermute | solution.py:265
  347.5 24.0 %collective-permute-start.25 = (f32[128,16,128]{2,1,0:T(8,128)S(1)}, f32[128,16,128]{2,1,0:T(8,128)S(1)}, u32[]{:S(2)}, u32[]{:S(2)}) collective-permute-start(f32[128,16,128]{2,1,0:T(8,128)S(1)} %get-tuple-element.92), channel_id=1, source_target_pairs={{0,1},{1,2},{2,3},{3,0},{4,5},{5,6},{6,7},{7,4},{8,9},{9,10},{10,1... | collective-permute-start | bytes 3145736 | tf_op jit(solution)/shard_map/ppermute | solution.py:252
  347.6 32.4 %collective-permute-start.24 = (f32[128,16,128]{2,1,0:T(8,128)S(1)}, f32[128,16,128]{2,1,0:T(8,128)S(1)}, u32[]{:S(2)}, u32[]{:S(2)}) collective-permute-start(f32[128,16,128]{2,1,0:T(8,128)S(1)} %get-tuple-element.92), channel_id=1, source_target_pairs={{1,0},{2,1},{3,2},{0,3},{5,4},{6,5},{7,6},{4,7},{9,8},{10,9},{11,1... | collective-permute-start | bytes 3145736 | tf_op jit(solution)/shard_map/ppermute | solution.py:253
  371.5 12.0 %collective-permute-start.26 = (f32[64,16,128]{2,1,0:T(8,128)S(1)}, f32[64,16,128]{2,1,0:T(8,128)S(1)}, u32[]{:S(2)}, u32[]{:S(2)}) collective-permute-start(f32[64,16,128]{2,1,0:T(8,128)S(1)} %slice.338), channel_id=1, source_target_pairs={{0,1},{1,2},{2,3},{3,0},{4,5},{5,6},{6,7},{7,4},{8,9},{9,10},{10,1... | collective-permute-start | bytes 1572872 | tf_op jit(solution)/shard_map/ppermute | solution.py:254
  380.0 11.5 %collective-permute-start.27 = (f32[64,16,128]{2,1,0:T(8,128)S(1)}, f32[64,16,128]{2,1,0:T(8,128)S(1)}, u32[]{:S(2)}, u32[]{:S(2)}) collective-permute-start(f32[64,16,128]{2,1,0:T(8,128)S(1)} %slice.339), channel_id=1, source_target_pairs={{1,0},{2,1},{3,2},{0,3},{5,4},{6,5},{7,6},{4,7},{9,8},{10,9},{11,1... | collective-permute-start | bytes 1572872 | tf_op jit(solution)/shard_map/ppermute | solution.py:255
  391.8 12.5 %copy-start = (f32[128,64,128]{2,1,0:T(8,128)}, f32[128,64,128]{2,1,0:T(8,128)S(1)}, u32[]{:S(2)}) copy-start(f32[128,64,128]{2,1,0:T(8,128)S(1)} %constant_dynamic-update-slice_fusion.f_ref) | copy-start | bytes 12582916
  391.9 11.4 %collective-permute-start.29 = (f32[16,64,128]{2,1,0:T(8,128)S(1)}, f32[16,64,128]{2,1,0:T(8,128)S(1)}, u32[]{:S(2)}, u32[]{:S(2)}) collective-permute-start(f32[16,64,128]{2,1,0:T(8,128)S(1)} %get-tuple-element.29), channel_id=1, source_target_pairs={{32,0},{36,4},{40,8},{44,12},{48,16},{52,20},{56,24},{60,28},{64,3... | collective-permute-start | bytes 1572872 | tf_op jit(solution)/shard_map/ppermute | solution.py:270
  393.2 11.0 %collective-permute-start.28 = (f32[16,64,128]{2,1,0:T(8,128)S(1)}, f32[16,64,128]{2,1,0:T(8,128)S(1)}, u32[]{:S(2)}, u32[]{:S(2)}) collective-permute-start(f32[16,64,128]{2,1,0:T(8,128)S(1)} %get-tuple-element.30), channel_id=1, source_target_pairs={{0,32},{4,36},{8,40},{12,44},{16,48},{20,52},{24,56},{28,60},{32,6... | collective-permute-start | bytes 1572872 | tf_op jit(solution)/shard_map/ppermute | solution.py:269
  403.3 23.1 %copy-start.9 = (f32[16,64,128]{2,1,0:T(8,128)}, f32[16,64,128]{2,1,0:T(8,128)S(1)}, u32[]{:S(2)}) copy-start(f32[16,64,128]{2,1,0:T(8,128)S(1)} %collective-permute-done.29.za_ref) | copy-start | bytes 1572868
  404.2 22.2 %copy-start.10 = (f32[16,64,128]{2,1,0:T(8,128)}, f32[16,64,128]{2,1,0:T(8,128)S(1)}, u32[]{:S(2)}) copy-start(f32[16,64,128]{2,1,0:T(8,128)S(1)} %collective-permute-done.28.zb_ref) | copy-start | bytes 1572868
  404.3 17.4 %collective-permute-start.30 = (f32[160,16,128]{2,1,0:T(8,128)S(1)}, f32[160,16,128]{2,1,0:T(8,128)S(1)}, u32[]{:S(2)}, u32[]{:S(2)}) collective-permute-start(f32[160,16,128]{2,1,0:T(8,128)S(1)} %pad_maximum_fusion.2), channel_id=1, source_target_pairs={{0,4},{4,8},{8,12},{12,16},{16,20},{20,24},{24,28},{32,36},{36,40}... | collective-permute-start | bytes 3932168 | tf_op jit(solution)/shard_map/ppermute | solution.py:275
  407.3 19.0 %collective-permute-start.31 = (f32[160,16,128]{2,1,0:T(8,128)S(1)}, f32[160,16,128]{2,1,0:T(8,128)}, u32[]{:S(2)}, u32[]{:S(2)}) collective-permute-start(f32[160,16,128]{2,1,0:T(8,128)S(1)} %pad_maximum_fusion.3), channel_id=1, source_target_pairs={{4,0},{8,4},{12,8},{16,12},{20,16},{24,20},{28,24},{36,32},{40,36}... | collective-permute-start | bytes 3932168 | tf_op jit(solution)/shard_map/ppermute | solution.py:276
  454.8 41.6 %collective-permute-start.37 = (f32[16,64,128]{2,1,0:T(8,128)S(1)}, f32[16,64,128]{2,1,0:T(8,128)S(1)}, u32[]{:S(2)}, u32[]{:S(2)}) collective-permute-start(f32[16,64,128]{2,1,0:T(8,128)S(1)} %get-tuple-element.21), channel_id=1, source_target_pairs={{32,0},{36,4},{40,8},{44,12},{48,16},{52,20},{56,24},{60,28},{64,3... | collective-permute-start | bytes 1572872 | tf_op jit(solution)/shard_map/ppermute | solution.py:270
  456.1 40.3 %collective-permute-start.36 = (f32[16,64,128]{2,1,0:T(8,128)S(1)}, f32[16,64,128]{2,1,0:T(8,128)S(1)}, u32[]{:S(2)}, u32[]{:S(2)}) collective-permute-start(f32[16,64,128]{2,1,0:T(8,128)S(1)} %get-tuple-element.22), channel_id=1, source_target_pairs={{0,32},{4,36},{8,40},{12,44},{16,48},{20,52},{24,56},{28,60},{32,6... | collective-permute-start | bytes 1572872 | tf_op jit(solution)/shard_map/ppermute | solution.py:269
  490.3 23.0 %collective-permute-start.33 = (f32[16,64,128]{2,1,0:T(8,128)}, f32[16,64,128]{2,1,0:T(8,128)}, u32[]{:S(2)}, u32[]{:S(2)}) collective-permute-start(f32[16,64,128]{2,1,0:T(8,128)} %get-tuple-element.25), channel_id=1, source_target_pairs={{32,0},{36,4},{40,8},{44,12},{48,16},{52,20},{56,24},{60,28},{64,3... | collective-permute-start | bytes 1572872 | tf_op jit(solution)/shard_map/ppermute | solution.py:270
  491.5 21.8 %collective-permute-start.32 = (f32[16,64,128]{2,1,0:T(8,128)}, f32[16,64,128]{2,1,0:T(8,128)}, u32[]{:S(2)}, u32[]{:S(2)}) collective-permute-start(f32[16,64,128]{2,1,0:T(8,128)} %get-tuple-element.26), channel_id=1, source_target_pairs={{0,32},{4,36},{8,40},{12,44},{16,48},{20,52},{24,56},{28,60},{32,6... | collective-permute-start | bytes 1572872 | tf_op jit(solution)/shard_map/ppermute | solution.py:269
  507.7 22.2 %collective-permute-start.39 = (f32[128,16,128]{2,1,0:T(8,128)S(1)}, f32[128,16,128]{2,1,0:T(8,128)}, u32[]{:S(2)}, u32[]{:S(2)}) collective-permute-start(f32[128,16,128]{2,1,0:T(8,128)S(1)} %get-tuple-element.19), channel_id=1, source_target_pairs={{4,0},{8,4},{12,8},{16,12},{20,16},{24,20},{28,24},{36,32},{40,36}... | collective-permute-start | bytes 3145736 | tf_op jit(solution)/shard_map/ppermute | solution.py:276
  509.6 20.3 %collective-permute-start.38 = (f32[128,16,128]{2,1,0:T(8,128)S(1)}, f32[128,16,128]{2,1,0:T(8,128)}, u32[]{:S(2)}, u32[]{:S(2)}) collective-permute-start(f32[128,16,128]{2,1,0:T(8,128)S(1)} %get-tuple-element.20), channel_id=1, source_target_pairs={{0,4},{4,8},{8,12},{12,16},{16,20},{20,24},{24,28},{32,36},{36,40}... | collective-permute-start | bytes 3145736 | tf_op jit(solution)/shard_map/ppermute | solution.py:275
  524.4 16.4 %collective-permute-start.35 = (f32[128,16,128]{2,1,0:T(8,128)}, f32[128,16,128]{2,1,0:T(8,128)}, u32[]{:S(2)}, u32[]{:S(2)}) collective-permute-start(f32[128,16,128]{2,1,0:T(8,128)} %get-tuple-element.23), channel_id=1, source_target_pairs={{4,0},{8,4},{12,8},{16,12},{20,16},{24,20},{28,24},{36,32},{40,36}... | collective-permute-start | bytes 3145736 | tf_op jit(solution)/shard_map/ppermute | solution.py:276
  526.3 15.7 %collective-permute-start.34 = (f32[128,16,128]{2,1,0:T(8,128)}, f32[128,16,128]{2,1,0:T(8,128)}, u32[]{:S(2)}, u32[]{:S(2)}) collective-permute-start(f32[128,16,128]{2,1,0:T(8,128)} %get-tuple-element.24), channel_id=1, source_target_pairs={{0,4},{4,8},{8,12},{12,16},{16,20},{20,24},{24,28},{32,36},{36,40}... | collective-permute-start | bytes 3145736 | tf_op jit(solution)/shard_map/ppermute | solution.py:275
  552.6 15.3 %copy-start.2 = (f32[4,128,16,128]{3,2,1,0:T(8,128)S(1)}, f32[4,128,16,128]{3,2,1,0:T(8,128)}, u32[]{:S(2)}) copy-start(f32[4,128,16,128]{3,2,1,0:T(8,128)} %back_xy.7) | copy-start | bytes 12582916
  554.4 13.5 %collective-permute-start.40 = (f32[64,16,128]{2,1,0:T(8,128)S(1)}, f32[64,16,128]{2,1,0:T(8,128)S(1)}, u32[]{:S(2)}, u32[]{:S(2)}) collective-permute-start(f32[64,16,128]{2,1,0:T(8,128)S(1)} %get-tuple-element.15), channel_id=1, source_target_pairs={{0,1},{1,2},{2,3},{3,0},{4,5},{5,6},{6,7},{7,4},{8,9},{9,10},{10,1... | collective-permute-start | bytes 1572872 | tf_op jit(solution)/shard_map/ppermute | solution.py:261
  554.5 13.4 %collective-permute-start.42 = (f32[64,16,128]{2,1,0:T(8,128)S(1)}, f32[64,16,128]{2,1,0:T(8,128)S(1)}, u32[]{:S(2)}, u32[]{:S(2)}) collective-permute-start(f32[64,16,128]{2,1,0:T(8,128)S(1)} %get-tuple-element.16), channel_id=1, source_target_pairs={{1,0},{2,1},{3,2},{0,3},{5,4},{6,5},{7,6},{4,7},{9,8},{10,9},{11,1... | collective-permute-start | bytes 1572872 | tf_op jit(solution)/shard_map/ppermute | solution.py:262
  568.2 25.3 %collective-permute-start.43 = (f32[128,16,128]{2,1,0:T(8,128)S(1)}, f32[128,16,128]{2,1,0:T(8,128)S(1)}, u32[]{:S(2)}, u32[]{:S(2)}) collective-permute-start(f32[128,16,128]{2,1,0:T(8,128)S(1)} %pad_maximum_fusion.7), channel_id=1, source_target_pairs={{1,0},{2,1},{3,2},{0,3},{5,4},{6,5},{7,6},{4,7},{9,8},{10,9},{11,1... | collective-permute-start | bytes 3145736 | tf_op jit(solution)/shard_map/ppermute | solution.py:265
  571.3 25.7 %collective-permute-start.41 = (f32[128,16,128]{2,1,0:T(8,128)S(1)}, f32[128,16,128]{2,1,0:T(8,128)S(1)}, u32[]{:S(2)}, u32[]{:S(2)}) collective-permute-start(f32[128,16,128]{2,1,0:T(8,128)S(1)} %pad_maximum_fusion.6), channel_id=1, source_target_pairs={{0,1},{1,2},{2,3},{3,0},{4,5},{5,6},{6,7},{7,4},{8,9},{9,10},{10,1... | collective-permute-start | bytes 3145736 | tf_op jit(solution)/shard_map/ppermute | solution.py:265
  616.0 23.9 %collective-permute-start.44 = (f32[16,8,16,128]{3,2,1,0:T(8,128)}, f32[16,8,16,128]{3,2,1,0:T(8,128)S(1)}, u32[]{:S(2)}, u32[]{:S(2)}) collective-permute-start(f32[16,8,16,128]{3,2,1,0:T(8,128)} %bitcast.152), channel_id=1, source_target_pairs={{1,0},{2,1},{3,2},{0,3},{5,4},{6,5},{7,6},{4,7},{9,8},{10,9},{11,1... | collective-permute-start | bytes 3145736 | tf_op jit(solution)/shard_map/ppermute | solution.py:253
  616.0 25.4 %collective-permute-start.45 = (f32[16,8,16,128]{3,2,1,0:T(8,128)}, f32[16,8,16,128]{3,2,1,0:T(8,128)S(1)}, u32[]{:S(2)}, u32[]{:S(2)}) collective-permute-start(f32[16,8,16,128]{3,2,1,0:T(8,128)} %bitcast.152), channel_id=1, source_target_pairs={{0,1},{1,2},{2,3},{3,0},{4,5},{5,6},{6,7},{7,4},{8,9},{9,10},{10,1... | collective-permute-start | bytes 3145736 | tf_op jit(solution)/shard_map/ppermute | solution.py:252
  640.0 11.7 %collective-permute-start.47 = (f32[8,8,16,128]{3,2,1,0:T(8,128)S(1)}, f32[8,8,16,128]{3,2,1,0:T(8,128)S(1)}, u32[]{:S(2)}, u32[]{:S(2)}) collective-permute-start(f32[8,8,16,128]{3,2,1,0:T(8,128)S(1)} %slice.364), channel_id=1, source_target_pairs={{1,0},{2,1},{3,2},{0,3},{5,4},{6,5},{7,6},{4,7},{9,8},{10,9},{11,1... | collective-permute-start | bytes 1572872 | tf_op jit(solution)/shard_map/ppermute | solution.py:255
  641.5 12.8 %collective-permute-start.46 = (f32[8,8,16,128]{3,2,1,0:T(8,128)S(1)}, f32[8,8,16,128]{3,2,1,0:T(8,128)S(1)}, u32[]{:S(2)}, u32[]{:S(2)}) collective-permute-start(f32[8,8,16,128]{3,2,1,0:T(8,128)S(1)} %slice.363), channel_id=1, source_target_pairs={{0,1},{1,2},{2,3},{3,0},{4,5},{5,6},{6,7},{7,4},{8,9},{9,10},{10,1... | collective-permute-start | bytes 1572872 | tf_op jit(solution)/shard_map/ppermute | solution.py:254
  (8 other events, 30.6 us)

commit v2 on v1

v2 whole, which is shorter than its diff:
```python
import functools

import jax
import jax.numpy as jnp
from jax import lax
from jax.experimental import pallas as pl
from jax.experimental.pallas import tpu as pltpu
from jax.sharding import PartitionSpec as P

ITERS = 2
VA = 4
RIM = 16
UNROLL = 4
BF = jnp.bfloat16
F32 = jnp.float32

COLS = 8
GROUPS = [list(range(8 * g, 8 * g + 8)) for g in range(4)]
Z_UP = [(8 * x + k, 8 * x + 8 + k) for x in range(3) for k in range(8)]
Z_DOWN = [(b, a) for a, b in Z_UP]
X_UP = [(8 * x + k, 8 * x + k + 1) for x in range(4) for k in range(7)]
X_DOWN = [(b, a) for a, b in X_UP]
V_UP = [(i, (i + 1) % 4) for i in range(4)]
V_DOWN = [(b, a) for a, b in V_UP]


def lateral_round(t):
    return [
        (4 * k + r, ((r + t + k // 2) % 4) * 8 + k) for k in range(8) for r in range(4)
    ]


def split(value):
    hi = value.astype(BF)
    lo = (value - hi.astype(F32)).astype(BF)
    return hi, lo


def band(kernel, length, extended):
    rim = RIM if extended else 0
    taps = kernel.shape[-1]
    row = jnp.arange(length)[:, None]
    col = jnp.arange(length + 2 * rim)[None, :]
    offset = col - row + (RIM - rim)
    hit = offset[:, :, None] == jnp.arange(taps)[None, None, :]
    return jnp.sum(jnp.where(hit, kernel[..., None, None, :], 0.0), axis=-1)


def edge_weights(kernel, positions, total):
    source = positions[:, None] + jnp.arange(kernel.shape[-1])[None, :] - RIM
    inside = (source >= 0) & (source < total)
    return jnp.sum(jnp.where(inside, kernel[..., None, :], 0.0), axis=-1)


def split_matrix(value):
    hi = lax.reduce_precision(value, 8, 7)
    return hi.astype(BF), (value - hi).astype(BF)


def left_form(matrix):
    hi, lo = split_matrix(matrix)
    return jnp.concatenate([hi, lo, hi], axis=-1)


def right_form(matrix):
    hi, lo = split_matrix(matrix)
    return jnp.concatenate([hi, lo, hi], axis=-2)


def dot(a, b):
    return lax.dot_general(a, b, (((1,), (0,)), ((), ())), preferred_element_type=F32)


def conv_rows(matrix, data):
    hi, lo = split(data)
    return dot(matrix, jnp.concatenate([hi, hi, lo], axis=0))


def conv_lanes(data, matrix):
    hi, lo = split(data)
    return dot(jnp.concatenate([hi, hi, lo], axis=1), matrix)


def xy_planes(load, mx, my, planes, mid_ref, finish):
    group = 2 * UNROLL
    steps = planes // group

    def along_x(i):
        for u in range(0, group, 2):
            p = group * i + u
            mid = conv_rows(mx, jnp.concatenate([load(p), load(p + 1)], axis=1))
            half = mid.shape[0]
            slot = lax.rem(i, 2)
            mid_ref[slot, u * half : (u + 1) * half] = mid[:, :128]
            mid_ref[slot, (u + 1) * half : (u + 2) * half] = mid[:, 128:]

    def along_y(i):
        done = conv_lanes(mid_ref[lax.rem(i, 2)], my)
        half = done.shape[0] // group
        for u in range(group):
            finish(group * i + u, done[u * half : (u + 1) * half])

    def body(i, _):
        along_y(i - 1)
        along_x(i)
        return 0

    along_x(0)
    lax.fori_loop(1, steps, body, 0)
    along_y(steps - 1)


def z_columns(load, mz, columns, store):
    def body(i, _):
        for u in range(UNROLL):
            x = 2 * (UNROLL * i + u)
            out = conv_rows(mz, jnp.concatenate([load(x), load(x + 1)], axis=1))
            store(x, out[:, :128])
            store(x + 1, out[:, 128:])
        return 0

    lax.fori_loop(0, columns // (2 * UNROLL), body, 0)


def each(count, step):
    def body(i, _):
        for u in range(UNROLL):
            step(UNROLL * i + u)
        return 0

    lax.fori_loop(0, count // UNROLL, body, 0)


def forward_kernel(
    mz_ref, mx_ref, my_ref, f_ref, zb_ref, za_ref, xl_ref, xr_ref, obs_ref,
    q_ref, first_ref, last_ref, e_ref, w_ref, mid_ref,
):
    depth, width = f_ref.shape[0], f_ref.shape[1]
    wide = width + 2 * RIM
    pitch = wide + 1
    part = width + 1
    mz = mz_ref[...]

    def middle(source, start):
        def step(z):
            e_ref[pl.ds((start + z) * pitch + RIM, width), :] = source[z]

        each(source.shape[0], step)

    def sides(z):
        e_ref[pl.ds(z * pitch, RIM), :] = xl_ref[z]
        e_ref[pl.ds(z * pitch + RIM + width, RIM), :] = xr_ref[z]

    middle(zb_ref, 0)
    middle(f_ref, RIM)
    middle(za_ref, RIM + depth)
    each(depth + 2 * RIM, sides)

    def load(x):
        return e_ref[pl.ds(x, depth + 2 * RIM, stride=pitch), :]

    def store(x, value):
        w_ref[pl.ds(x, depth, stride=pitch), :] = value

    z_columns(load, mz, wide, store)

    def finish(p, blurred):
        q_ref[pl.ds(p * part, width), :] = obs_ref[p] / blurred

    xy_planes(
        lambda p: w_ref[pl.ds(p * pitch, wide), :], mx_ref[...], my_ref[...], depth, mid_ref, finish
    )

    def edges(z):
        first_ref[z] = q_ref[pl.ds(z * part, width), :]
        last_ref[z] = q_ref[pl.ds((depth - RIM + z) * part, width), :]

    each(RIM, edges)


def back_z_kernel(mz_ref, q_ref, zb_ref, za_ref, r_ref, first_ref, last_ref, b_ref, a_ref):
    width = zb_ref.shape[1]
    part = width + 1
    depth = q_ref.shape[0] // part

    def rims(z):
        b_ref[pl.ds(z * part, width), :] = zb_ref[z]
        a_ref[pl.ds(z * part, width), :] = za_ref[z]

    each(RIM, rims)

    def load(x):
        return jnp.concatenate(
            [
                b_ref[pl.ds(x, RIM, stride=part), :],
                q_ref[pl.ds(x, depth, stride=part), :],
                a_ref[pl.ds(x, RIM, stride=part), :],
            ],
            axis=0,
        )

    def store(x, value):
        r_ref[pl.ds(x, depth, stride=part), :] = value

    z_columns(load, mz_ref[...], width, store)

    def edges(z):
        first_ref[z] = r_ref[pl.ds(z * part, RIM), :]
        last_ref[z] = r_ref[pl.ds(z * part + width - RIM, RIM), :]

    each(depth, edges)


def back_xy_kernel(me_ref, w_ref, mx_ref, my_ref, r_ref, xl_ref, xr_ref, *rest):
    acc_ref, l_ref, mid_ref = rest if len(rest) == 3 else (None, *rest)
    me = me_ref[0]
    depth = xl_ref.shape[0]
    part = r_ref.shape[0] // depth

    def load(p):
        return jnp.concatenate(
            [xl_ref[p], r_ref[pl.ds(p * part, part - 1), :], xr_ref[p]], axis=0
        )

    def finish(p, back):
        term = w_ref[lax.div(p, 16)] * jnp.log(back)
        for quarter in range(4):
            slot = lax.rem(quarter - me + 4, 4)
            piece = term[quarter * 16 : quarter * 16 + 16]
            if acc_ref is not None:
                piece = piece + acc_ref[slot, p]
            l_ref[slot, p] = piece

    xy_planes(load, mx_ref[...], my_ref[...], depth, mid_ref, finish)


def assemble_kernel(at_ref, *refs):
    *pieces, block_ref, first_ref, last_ref = refs
    depth, narrow = pieces[0].shape[0], pieces[0].shape[1]
    for number, piece in enumerate(pieces):
        at = pl.multiple_of(at_ref[number], narrow)

        def step(z):
            block_ref[z, pl.ds(at, narrow), :] = piece[z]

        each(depth, step)
    first_ref[...] = block_ref[:RIM]
    last_ref[...] = block_ref[depth - RIM :]


VMEM = pl.BlockSpec(memory_space=pltpu.VMEM)
SMEM = pl.BlockSpec(memory_space=pltpu.SMEM)


def params(mebibytes):
    return pltpu.CompilerParams(vmem_limit_bytes=mebibytes * 2**20)


def forward(mz, mx, my, f, zb, za, xl, xr, obs):
    depth, width, lines = f.shape
    rim = jax.ShapeDtypeStruct((RIM, width, lines), F32)
    pitch = width + 2 * RIM + 1
    return pl.pallas_call(
        forward_kernel,
        in_specs=[VMEM] * 9,
        out_specs=[VMEM] * 3,
        out_shape=[jax.ShapeDtypeStruct((depth * (width + 1), lines), F32), rim, rim],
        scratch_shapes=[
            pltpu.VMEM(((depth + 2 * RIM) * pitch, lines), F32),
            pltpu.VMEM((depth * pitch, lines), F32),
            pltpu.VMEM((2, 2 * UNROLL * width, lines), F32),
        ],
        compiler_params=params(20),
        cost_estimate=pl.CostEstimate(flops=10**10, bytes_accessed=2 * 10**7, transcendentals=0),
        name="forward",
    )(mz, mx, my, f, zb, za, xl, xr, obs)


def back_z(mz, q, zb, za):
    width, lines = zb.shape[1:]
    depth = q.shape[0] // (width + 1)
    rim = jax.ShapeDtypeStruct((depth, RIM, lines), F32)
    padded = pltpu.VMEM((RIM * (width + 1), lines), F32)
    return pl.pallas_call(
        back_z_kernel,
        in_specs=[VMEM] * 4,
        out_specs=[VMEM] * 3,
        out_shape=[jax.ShapeDtypeStruct(q.shape, F32), rim, rim],
        scratch_shapes=[padded, padded],
        compiler_params=params(12),
        cost_estimate=pl.CostEstimate(flops=3 * 10**9, bytes_accessed=10**7, transcendentals=0),
        name="back_z",
    )(mz, q, zb, za)


def back_xy(me, weight, mx, my, r, xl, xr, acc=None):
    depth, _, lines = xl.shape
    width = r.shape[0] // depth - 1
    args = [me, weight, mx, my, r, xl, xr] + ([] if acc is None else [acc])
    return pl.pallas_call(
        back_xy_kernel,
        in_specs=[SMEM, SMEM] + [VMEM] * (len(args) - 2),
        out_specs=VMEM,
        out_shape=jax.ShapeDtypeStruct((4, depth, width // 4, lines), F32),
        scratch_shapes=[pltpu.VMEM((2, 2 * UNROLL * width, lines), F32)],
        compiler_params=params(12),
        cost_estimate=pl.CostEstimate(flops=5 * 10**9, bytes_accessed=10**7, transcendentals=10**6),
        name="back_xy",
    )(*args)


def assemble(at, pieces):
    depth, narrow, lines = pieces[0].shape
    width = narrow * len(pieces)
    rim = jax.ShapeDtypeStruct((RIM, width, lines), F32)
    return pl.pallas_call(
        assemble_kernel,
        in_specs=[SMEM] + [VMEM] * len(pieces),
        out_specs=[VMEM] * 3,
        out_shape=[jax.ShapeDtypeStruct((depth, width, lines), F32), rim, rim],
        compiler_params=params(6),
        cost_estimate=pl.CostEstimate(flops=10**6, bytes_accessed=10**7, transcendentals=0),
        name="assemble",
    )(at.astype(jnp.int32), *pieces)


def gather_quarters(quarter, half):
    below = lax.ppermute(quarter, "view", V_UP)
    above = lax.ppermute(quarter, "view", V_DOWN)
    first = lax.ppermute(below[:half], "view", V_UP)
    second = lax.ppermute(above[half:], "view", V_DOWN)
    return quarter, above, jnp.concatenate([first, second], axis=0), below


def scatter_quarters(parts):
    half = parts.shape[1] // 2
    first = lax.ppermute(parts[2, :half], "view", V_UP)
    second = lax.ppermute(parts[2, half:], "view", V_DOWN)
    up = jnp.concatenate([parts[1, :half] + first, parts[1, half:]], axis=0)
    down = jnp.concatenate([parts[3, :half], parts[3, half:] + second], axis=0)
    return parts[0] + lax.ppermute(up, "view", V_UP) + lax.ppermute(down, "view", V_DOWN)


def to_blocks(value):
    return lax.all_to_all(
        value, "owner", split_axis=1, concat_axis=0, axis_index_groups=GROUPS, tiled=True
    )


def z_rims(first, last):
    before = lax.ppermute(last, "owner", Z_UP)
    after = lax.ppermute(first, "owner", Z_DOWN)
    return before, after


def x_rims(first, last):
    left = lax.ppermute(last, "owner", X_UP)
    right = lax.ppermute(first, "owner", X_DOWN)
    return left, right


def local(estimate, axial_views, lateral_views, psf_axial, psf_lateral, coverage):
    slab, lines, columns = estimate.shape
    owner = lax.axis_index("owner")
    me = lax.axis_index("view")
    k = owner % 8
    z_chip = owner // 8
    width = columns // COLS
    depth = 8 * slab

    turned = estimate.transpose(0, 2, 1).reshape(slab, COLS, 4, width // 4, lines)
    mine = lax.dynamic_index_in_dim(turned, me, 2, keepdims=False)
    cover = jnp.repeat(coverage[0].astype(F32), 2, axis=0)
    cover = jnp.pad(cover[:, None, :], ((0, 0), (0, width // 4 - 1), (0, lines - cover.shape[1])))
    mine = jnp.concatenate([mine, cover[None]], axis=0).reshape(slab + 1, -1, lines)
    axial_views, mine = lax.optimization_barrier((axial_views, mine))
    got = to_blocks(mine).reshape(8, slab + 1, width // 4, lines)
    axial_turned = axial_views[0].transpose(0, 2, 1)
    lateral_views, axial_turned, got = lax.optimization_barrier(
        (lateral_views, axial_turned, got)
    )
    axial = to_blocks(axial_turned)
    quarter = got[:, :slab].reshape(depth, width // 4, lines)
    cover = got[:, slab, 0, :8]

    chunks = lateral_views[0].transpose(2, 0, 1).reshape(4, depth, slab, lines)
    pieces, places = [], []
    for t in range(4):
        target = (owner % 4 + t + z_chip) % 4
        piece = lax.dynamic_index_in_dim(chunks, target, 0, keepdims=False)
        pieces.append(lax.ppermute(piece, "owner", lateral_round(t)))
        places.append(((z_chip - t - k // 2) % 4) * slab)
    lateral = assemble(jnp.stack(places), pieces)[0]

    count = jnp.sum(cover, axis=-1)
    weight_axial = lax.dynamic_index_in_dim(cover, me, 1, keepdims=False)
    weight_lateral = lax.dynamic_index_in_dim(cover, VA + me, 1, keepdims=False)

    taps = jnp.concatenate([psf_axial, psf_lateral], axis=0)
    taps = taps / jnp.sum(taps, axis=-1, keepdims=True)
    flipped = taps[..., ::-1]
    z_at = z_chip * depth + jnp.arange(depth)
    x_at = k * width + jnp.arange(width)
    y_at = jnp.arange(lines)
    ahead_z = left_form(band(taps[:, 0], depth, True))
    ahead_x = left_form(band(taps[:, 2], width, True))
    ahead_y = right_form(jnp.swapaxes(band(taps[:, 1], lines, False), 1, 2))
    wz = edge_weights(flipped[:, 0], z_at, 4 * depth)
    wx = edge_weights(flipped[:, 2], x_at, columns)
    wy = edge_weights(flipped[:, 1], y_at, lines)
    back_mz = left_form(band(flipped[:, 0], depth, True) / wz[:, :, None])
    back_mx = left_form(band(flipped[:, 2], width, True) / wx[:, :, None])
    back_my = right_form(
        jnp.swapaxes(band(flipped[:, 1], lines, False) / wy[:, :, None], 1, 2)
    )
    me_arr = me[None].astype(jnp.int32)

    for iteration in range(ITERS):
        pieces = gather_quarters(quarter, depth // 2)
        places = ((me + jnp.arange(4)) % 4) * (width // 4)
        block, first, last = assemble(places, pieces)
        before, after = z_rims(first, last)
        long_right = jnp.concatenate(
            [before[:, -RIM:], block[:, -RIM:], after[:, -RIM:]], axis=0
        )
        long_left = jnp.concatenate(
            [before[:, :RIM], block[:, :RIM], after[:, :RIM]], axis=0
        )
        left, right = x_rims(long_left, long_right)
        logs = None
        for number, (obs, weight) in enumerate(
            ((axial, weight_axial), (lateral, weight_lateral))
        ):
            quotient, first, last = forward(
                ahead_z[number], ahead_x[number], ahead_y[number],
                block, before, after, left, right, obs,
            )
            rz, low, high = back_z(back_mz[number], quotient, *z_rims(first, last))
            logs = back_xy(
                me_arr, weight, back_mx[number], back_my[number],
                rz, *x_rims(low, high), acc=logs,
            )
        total = scatter_quarters(logs)
        slabs = total.reshape(8, slab, width // 4, lines) / count[:, None, None, None]
        quarter = quarter * jnp.exp(slabs.reshape(quarter.shape))

    slabs = lax.all_to_all(
        quarter, "owner", split_axis=0, concat_axis=1, axis_index_groups=GROUPS, tiled=True
    )
    slabs = slabs.reshape(slab, COLS, width // 4, lines)
    pieces = gather_quarters(slabs, slab // 2)
    result = jnp.zeros((slab, COLS, 4, width // 4, lines), F32)
    for d in range(4):
        result = lax.dynamic_update_index_in_dim(result, pieces[d], (me + d) % 4, axis=2)
    return result.reshape(slab, columns, lines).transpose(0, 2, 1)


def solution(mesh):
    in_specs = (
        P("owner", None, None),
        P("view", "owner", None, None),
        P("view", "owner", None, None),
        P("view", None, None),
        P("view", None, None),
        P("owner", None, None),
    )
    out_specs = P("owner", None, None)
    return jax.shard_map(local, mesh=mesh, in_specs=in_specs, out_specs=out_specs, check_vma=False)
```

time: 672 us -> 612 us (0.911)
  Pallas kernels: 182 us -> 96.9 us
  waiting for transfers between devices: 198 us -> 254 us
  local copies, waits for them, and re-layouts: 88.6 us -> 63.9 us
  starting transfers between devices: 154 us -> 134 us
  other arithmetic: 20.5 us -> 30 us
  blocking collectives: 17.5 us -> 27 us
    pallas_call x12 -> x15, Pallas kernels: 182 us -> 96.9 us  [the longest x4 47.6 us: forward(): pl.pallas_call(forward_kernel, in_specs=[VMEM] * 9, out_specs=[VMEM] * 3,...]
    ppermute x28, waiting for transfers between devices: 40 us -> 124 us  [the longest x6 50.7 us: z_rims(): after = lax.ppermute(first, 'owner', Z_DOWN)]
    ppermute x2, waiting for transfers between devices: 43.4 us -> 1 us  [scatter_quarters(): lax.ppermute(down, 'view', V_DOWN)]
    ppermute x3, waiting for transfers between devices: 30.8 us -> 0.17 us  [gather_quarters(): above = lax.ppermute(quarter, 'view', V_DOWN)]
    ppermute x2, waiting for transfers between devices: 6.72 us -> 29.6 us  [scatter_quarters(): lax.ppermute(up, 'view', V_UP)]
    ppermute x3, waiting for transfers between devices: 30 us -> 51 us  [gather_quarters(): below = lax.ppermute(quarter, 'view', V_UP)]
    slice x10 -> x2, local copies, waits for them, and re-layouts: 16.9 us -> 0.19 us  [local(): quarter = got[:, :slab].reshape(depth, width // 4, lines)]
    all_to_all x3 -> x2, starting transfers between devices: 28.9 us -> 12.7 us  [to_blocks(): lax.all_to_all(value, 'owner', split_axis=1, concat_axis=0, axis_index_gr...]
  transfers between devices with their start and end apart: 51 -> 50, of which waited for: 23 -> 24; matrix products, arithmetic and copies ran while one was open for 12% -> 10% of each run, Pallas kernels for 20% -> 9%
where the time goes in v2:
time: 612 us; the launch traced here: 607 us
  waiting for transfers between devices  254 us (42%)
  starting transfers between devices  134 us (22%)
  Pallas kernels  96.9 us (16%)
  local copies, waits for them, and re-layouts  63.9 us (10%)
  other arithmetic  30 us (5%)
  blocking collectives  27 us (4%)
    ppermute x3, waiting for transfers between devices, gather_quarters(): below = lax.ppermute(quarter, 'view', V_UP)  51 us
    ppermute x6, waiting for transfers between devices, z_rims(): after = lax.ppermute(first, 'owner', Z_DOWN)  50.7 us
    pallas_call x4, Pallas kernels, forward(): pl.pallas_call(forward_kernel, in_specs=[VMEM] * 9, out_specs=[VMEM] * 3,...  47.6 us
    ppermute x4, waiting for transfers between devices, local(): pieces.append(lax.ppermute(piece, 'owner', lateral_round(t)))  38.5 us
    ppermute x6, starting transfers between devices, x_rims(): left = lax.ppermute(last, 'owner', X_UP)  34.2 us
    ppermute x2, waiting for transfers between devices, scatter_quarters(): lax.ppermute(up, 'view', V_UP)  29.6 us
    pallas_call x4, Pallas kernels, back_xy(): pl.pallas_call(back_xy_kernel, in_specs=[SMEM, SMEM] + [VMEM] * (len(args...  27.3 us
    all_to_all x1, blocking collectives, local(): lax.all_to_all(quarter, 'owner', split_axis=0, concat_axis=1, axis_index_...  27 us
  transfers between devices with their start and end apart: 50, of which 24 were waited for; matrix products, arithmetic and copies ran while one was open for 10% of the time, Pallas kernels for 9%

profile of v2, /device:TPU:1, one launch (start us, length us, event | category | flops | bytes accessed | tf_op | source)
XLA Modules:
  0.0 607.3 jit_solution(10671842958040829500)
XLA Ops:
  0.0 5.3 copy.87
  8.6 6.8 %all-to-all-start = ((f32[17,128,128]{2,0,1:T(8,128)}), f32[17,128,128]{2,0,1:T(8,128)S(1)}, u32[]{:S(2)}, u32[]{:S(2)}) async-start(f32[17,128,128]{2,0,1:T(8,128)} %copy.90), calls=%async_computation | async-start | bytes 3145728 | tf_op jit(solution)/shard_map/all_to_all | solution.py:345
  18.3 5.5 copy.89
  26.7 9.3 %all-to-all-done = f32[17,128,128]{2,0,1:T(8,128)S(1)} async-done(((f32[17,128,128]{2,0,1:T(8,128)}), f32[17,128,128]{2,0,1:T(8,128)S(1)}, u32[]{:S(2)}, u32[]{:S(2)}) %all-to-all-start) | async-done | bytes 1114144 | tf_op jit(solution)/shard_map/all_to_all | solution.py:345
  42.3 5.9 all-to-all-start.1
  53.2 9.2 %collective-permute-done.1.refs_3_ = f32[128,16,128]{2,1,0:T(8,128)S(1)} collective-permute-done((f32[128,16,128]{2,1,0:T(8,128)S(1)}, f32[128,16,128]{2,1,0:T(8,128)S(1)}, u32[]{:S(2)}, u32[]{:S(2)}) %collective-permute-start.1) | collective-permute-done | bytes 1048608 | tf_op jit(solution)/shard_map/ppermute | solution.py:328
  64.1 2.7 collective-permute-start.3
  72.2 4.4 collective-permute-done.2
  77.9 2.3 assemble.3
  83.0 3.1 collective-permute-start.4
  86.2 5.5 copy.114
  91.6 4.4 dynamic-slice_bitcast_fusion
  96.0 5.0 collective-permute-start.10
  102.6 38.2 %collective-permute-done.5.za_ref = f32[16,64,128]{2,1,0:T(8,128)S(1)} collective-permute-done((f32[16,64,128]{2,1,0:T(8,128)S(1)}, f32[16,64,128]{2,1,0:T(8,128)S(1)}, u32[]{:S(2)}, u32[]{:S(2)}) %collective-permute-start.5) | collective-permute-done | bytes 524320 | tf_op jit(solution)/shard_map/ppermute | solution.py:352
  142.8 2.4 collective-permute-start.7
  146.4 3.1 collective-permute-start.6
  151.5 2.3 collective-permute-start.11
  153.8 3.0 collective-permute-start.8
  165.2 36.7 %collective-permute-done.11.refs_3_ = f32[128,16,128]{2,1,0:T(8,128)S(1)} collective-permute-done((f32[128,16,128]{2,1,0:T(8,128)}, f32[128,16,128]{2,1,0:T(8,128)S(1)}, u32[]{:S(2)}, u32[]{:S(2)}) %collective-permute-start.11) | collective-permute-done | bytes 1048608 | tf_op jit(solution)/shard_map/ppermute | solution.py:391
  204.3 3.5 assemble.4
  209.8 3.6 copy.108
  213.5 13.8 %forward.5 = (f32[8320,128]{1,0:T(8,128)S(1)}, f32[16,64,128]{2,1,0:T(8,128)S(1)}, f32[16,64,128]{2,1,0:T(8,128)S(1)}) custom-call(bf16[128,480]{1,0:T(8,128)(2,1)S(1)} %get-tuple-element.115.mz_ref, bf16[64,288]{1,0:T(8,128)(2,1)S(1)} %copy-done.11, bf16[384,128]{1,0:T(8,128)(2,1)S(1)} %copy-done.10, f32[128,64,128]{2,1,0:T(8,128)S(1)} %copy-done.5, ...), custom_call_target="tpu_custom_call" | custom-call | flops 10000000000 | bytes 20000000 | tf_op jit(solution)/shard_map/forward/pallas_call | solution.py:263
  230.0 12.4 %forward.4 = (f32[8320,128]{1,0:T(8,128)S(1)}, f32[16,64,128]{2,1,0:T(8,128)S(1)}, f32[16,64,128]{2,1,0:T(8,128)S(1)}) custom-call(bf16[128,480]{1,0:T(8,128)(2,1)S(1)} %get-tuple-element.116.mz_ref, bf16[64,288]{1,0:T(8,128)(2,1)S(1)} %get-tuple-element.132.mx_ref, bf16[384,128]{1,0:T(8,128)(2,1)S(1)} %get-tuple-element.124.my_ref, ...), custom_call_target="tpu_custom_call" | custom-call | flops 10000000000 | bytes 20000000 | tf_op jit(solution)/shard_map/forward/pallas_call | solution.py:263
  242.4 8.1 %collective-permute-start.12 = (f32[16,64,128]{2,1,0:T(8,128)S(1)}, f32[16,64,128]{2,1,0:T(8,128)S(1)}, u32[]{:S(2)}, u32[]{:S(2)}) collective-permute-start(f32[16,64,128]{2,1,0:T(8,128)S(1)} %get-tuple-element.50), channel_id=1, source_target_pairs={{0,32},{4,36},{8,40},{12,44},{16,48},{20,52},{24,56},{28,60},{32,6... | collective-permute-start | bytes 1572872 | tf_op jit(solution)/shard_map/ppermute | solution.py:351
  252.0 4.2 back_z.5
  260.2 3.4 collective-permute-start.19
  263.7 4.5 back_z.4
  270.2 6.0 collective-permute-start.14
  281.7 7.3 %back_xy.4.rest_0_ = f32[4,128,16,128]{3,2,1,0:T(8,128)S(1)} custom-call(s32[1]{0:T(128)} %bitcast.11.me_ref, f32[8]{0:T(128)S(1)} %get-tuple-element.83.w_ref, bf16[64,288]{1,0:T(8,128)(2,1)S(1)} %get-tuple-element.133.mx_ref, bf16[384,128]{1,0:T(8,128)(2,1)S(1)} %get-tuple-element.125.my_ref, f32[8320,128]{1,0:T(8,128)S(1)} %copy-done.22, ...), custom_call_target="tpu_custom_call" | custom-call | flops 5000000000 | bytes 10000000 | tf_op jit(solution)/shard_map/back_xy/pallas_call | solution.py:300
  289.1 3.6 collective-permute-done.15.xr_ref
  292.7 7.3 %back_xy.5 = f32[4,128,16,128]{3,2,1,0:T(8,128)S(1)} custom-call(s32[1]{0:T(128)} %bitcast.11.me_ref, f32[8]{0:T(128)S(1)} %get-tuple-element.84.w_ref, bf16[64,288]{1,0:T(8,128)(2,1)S(1)} %get-tuple-element.134.mx_ref, bf16[384,128]{1,0:T(8,128)(2,1)S(1)} %get-tuple-element.126.my_ref, f32[8320,128]{1,0:T(8,128)S(1)} %bitcast.164, ...), custom_call_target="tpu_custom_call" | custom-call | flops 5000000000 | bytes 10000000 | tf_op jit(solution)/shard_map/back_xy/pallas_call | solution.py:300
  301.2 2.2 collective-permute-start.22
  303.5 7.1 %collective-permute-done.20 = f32[64,16,128]{2,1,0:T(8,128)S(1)} collective-permute-done((f32[64,16,128]{2,1,0:T(8,128)S(1)}, f32[64,16,128]{2,1,0:T(8,128)S(1)}, u32[]{:S(2)}, u32[]{:S(2)}) %collective-permute-start.20) | collective-permute-done | bytes 524320 | tf_op jit(solution)/shard_map/ppermute | solution.py:337
  315.7 16.8 %collective-permute-done.21 = f32[128,16,128]{2,1,0:T(8,128)} collective-permute-done((f32[128,16,128]{2,1,0:T(8,128)}, f32[128,16,128]{2,1,0:T(8,128)}, u32[]{:S(2)}, u32[]{:S(2)}) %collective-permute-start.21) | collective-permute-done | bytes 1048608 | tf_op jit(solution)/shard_map/ppermute | solution.py:341
  338.4 19.2 %collective-permute-done.25.refs_3_ = f32[128,16,128]{2,1,0:T(8,128)S(1)} collective-permute-done((f32[128,16,128]{2,1,0:T(8,128)S(1)}, f32[128,16,128]{2,1,0:T(8,128)S(1)}, u32[]{:S(2)}, u32[]{:S(2)}) %collective-permute-start.25) | collective-permute-done | bytes 1048608 | tf_op jit(solution)/shard_map/ppermute | solution.py:328
  360.7 8.9 %collective-permute-done.26 = f32[64,16,128]{2,1,0:T(8,128)S(1)} collective-permute-done((f32[64,16,128]{2,1,0:T(8,128)S(1)}, f32[64,16,128]{2,1,0:T(8,128)S(1)}, u32[]{:S(2)}, u32[]{:S(2)}) %collective-permute-start.26) | collective-permute-done | bytes 524320 | tf_op jit(solution)/shard_map/ppermute | solution.py:330
  371.8 4.0 collective-permute-start.28
  377.3 8.3 %collective-permute-done.28.zb_ref = f32[16,64,128]{2,1,0:T(8,128)S(1)} collective-permute-done((f32[16,64,128]{2,1,0:T(8,128)S(1)}, f32[16,64,128]{2,1,0:T(8,128)S(1)}, u32[]{:S(2)}, u32[]{:S(2)}) %collective-permute-start.28) | collective-permute-done | bytes 524320 | tf_op jit(solution)/shard_map/ppermute | solution.py:351
  385.6 12.5 %collective-permute-done.29.za_ref = f32[16,64,128]{2,1,0:T(8,128)S(1)} collective-permute-done((f32[16,64,128]{2,1,0:T(8,128)S(1)}, f32[16,64,128]{2,1,0:T(8,128)S(1)}, u32[]{:S(2)}, u32[]{:S(2)}) %collective-permute-start.29) | collective-permute-done | bytes 524320 | tf_op jit(solution)/shard_map/ppermute | solution.py:352
  398.2 3.4 collective-permute-start.31
  401.8 8.8 %collective-permute-start.30 = (f32[160,16,128]{2,1,0:T(8,128)S(1)}, f32[160,16,128]{2,1,0:T(8,128)S(1)}, u32[]{:S(2)}, u32[]{:S(2)}) collective-permute-start(f32[160,16,128]{2,1,0:T(8,128)S(1)} %pad_maximum_fusion.2), channel_id=1, source_target_pairs={{0,4},{4,8},{8,12},{12,16},{16,20},{20,24},{24,28},{32,36},{36,40}... | collective-permute-start | bytes 3932168 | tf_op jit(solution)/shard_map/ppermute | solution.py:357
  410.6 12.8 %collective-permute-done.31.xr_ref = f32[160,16,128]{2,1,0:T(8,128)S(1)} collective-permute-done((f32[160,16,128]{2,1,0:T(8,128)S(1)}, f32[160,16,128]{2,1,0:T(8,128)S(1)}, u32[]{:S(2)}, u32[]{:S(2)}) %collective-permute-start.31) | collective-permute-done | bytes 1310752 | tf_op jit(solution)/shard_map/ppermute | solution.py:358
  424.9 10.7 %forward.7 = (f32[8320,128]{1,0:T(8,128)S(1)}, f32[16,64,128]{2,1,0:T(8,128)S(1)}, f32[16,64,128]{2,1,0:T(8,128)S(1)}) custom-call(bf16[128,480]{1,0:T(8,128)(2,1)S(1)} %get-tuple-element.115.mz_ref, bf16[64,288]{1,0:T(8,128)(2,1)S(1)} %copy-done.11, bf16[384,128]{1,0:T(8,128)(2,1)S(1)} %copy-done.10, f32[128,64,128]{2,1,0:T(8,128)S(1)} %get-tuple-element.62.f_ref, ...), custom_call_target="tpu_custom_call" | custom-call | flops 10000000000 | bytes 20000000 | tf_op jit(solution)/shard_map/forward/pallas_call | solution.py:263
  435.6 3.4 collective-permute-start.36
  440.3 10.7 %forward.6 = (f32[8320,128]{1,0:T(8,128)S(1)}, f32[16,64,128]{2,1,0:T(8,128)S(1)}, f32[16,64,128]{2,1,0:T(8,128)S(1)}) custom-call(bf16[128,480]{1,0:T(8,128)(2,1)S(1)} %get-tuple-element.116.mz_ref, bf16[64,288]{1,0:T(8,128)(2,1)S(1)} %get-tuple-element.132.mx_ref, bf16[384,128]{1,0:T(8,128)(2,1)S(1)} %get-tuple-element.124.my_ref, ...), custom_call_target="tpu_custom_call" | custom-call | flops 10000000000 | bytes 20000000 | tf_op jit(solution)/shard_map/forward/pallas_call | solution.py:263
  451.0 4.0 collective-permute-start.32
  456.3 3.1 back_z.7
  459.4 5.2 collective-permute-start.38
  466.6 3.1 back_z.6
  469.7 9.2 %collective-permute-start.34 = (f32[128,16,128]{2,1,0:T(8,128)S(1)}, f32[128,16,128]{2,1,0:T(8,128)S(1)}, u32[]{:S(2)}, u32[]{:S(2)}) collective-permute-start(f32[128,16,128]{2,1,0:T(8,128)S(1)} %get-tuple-element.69), channel_id=1, source_target_pairs={{0,4},{4,8},{8,12},{12,16},{16,20},{20,24},{24,28},{32,36},{36,40}... | collective-permute-start | bytes 3145736 | tf_op jit(solution)/shard_map/ppermute | solution.py:357
  480.9 6.3 %back_xy.6.rest_0_ = f32[4,128,16,128]{3,2,1,0:T(8,128)S(1)} custom-call(s32[1]{0:T(128)} %bitcast.11.me_ref, f32[8]{0:T(128)S(1)} %get-tuple-element.83.w_ref, bf16[64,288]{1,0:T(8,128)(2,1)S(1)} %get-tuple-element.133.mx_ref, bf16[384,128]{1,0:T(8,128)(2,1)S(1)} %get-tuple-element.125.my_ref, f32[8320,128]{1,0:T(8,128)S(1)} %get-tuple-element.74.r_ref, ...), custom_call_target="tpu_custom_call" | custom-call | flops 5000000000 | bytes 10000000 | tf_op jit(solution)/shard_map/back_xy/pallas_call | solution.py:300
  487.2 3.4 collective-permute-done.34.xl_ref
  490.6 4.7 collective-permute-done.35.xr_ref
  495.3 6.3 %back_xy.7 = f32[4,128,16,128]{3,2,1,0:T(8,128)S(1)} custom-call(s32[1]{0:T(128)} %bitcast.11.me_ref, f32[8]{0:T(128)S(1)} %get-tuple-element.84.w_ref, bf16[64,288]{1,0:T(8,128)(2,1)S(1)} %get-tuple-element.134.mx_ref, bf16[384,128]{1,0:T(8,128)(2,1)S(1)} %get-tuple-element.126.my_ref, f32[8320,128]{1,0:T(8,128)S(1)} %get-tuple-element.68.r_ref, ...), custom_call_target="tpu_custom_call" | custom-call | flops 5000000000 | bytes 10000000 | tf_op jit(solution)/shard_map/back_xy/pallas_call | solution.py:300
  501.9 2.7 collective-permute-start.42
  504.5 12.5 %collective-permute-done.40 = f32[64,16,128]{2,1,0:T(8,128)S(1)} collective-permute-done((f32[64,16,128]{2,1,0:T(8,128)S(1)}, f32[64,16,128]{2,1,0:T(8,128)S(1)}, u32[]{:S(2)}, u32[]{:S(2)}) %collective-permute-start.40) | collective-permute-done | bytes 524320 | tf_op jit(solution)/shard_map/ppermute | solution.py:337
  517.8 2.3 collective-permute-start.43
  520.1 12.7 %collective-permute-done.41 = f32[128,16,128]{2,1,0:T(8,128)S(1)} collective-permute-done((f32[128,16,128]{2,1,0:T(8,128)S(1)}, f32[128,16,128]{2,1,0:T(8,128)S(1)}, u32[]{:S(2)}, u32[]{:S(2)}) %collective-permute-start.41) | collective-permute-done | bytes 1048608 | tf_op jit(solution)/shard_map/ppermute | solution.py:341
  533.2 27.0 %all_to_all.48 = f32[128,16,128]{2,1,0:T(8,128)S(1)} all-to-all(f32[128,16,128]{2,1,0:T(8,128)S(1)} %fusion.4), channel_id=1, replica_groups={{0,4,8,12,16,20,24,28},{32,36,40,44,48,52,56,60},{64,68,72,76,80,84,88,..., dimensions={0} | all-to-all | bytes 2097152 | tf_op jit(solution)/shard_map/all_to_all | solution.py:447
  564.1 22.6 %collective-permute-done.45 = f32[16,8,16,128]{3,2,1,0:T(8,128)S(1)} collective-permute-done((f32[16,8,16,128]{3,2,1,0:T(8,128)}, f32[16,8,16,128]{3,2,1,0:T(8,128)S(1)}, u32[]{:S(2)}, u32[]{:S(2)}) %collective-permute-start.45) | collective-permute-done | bytes 1048608 | tf_op jit(solution)/shard_map/ppermute | solution.py:328
  586.8 2.7 collective-permute-start.47
  589.6 2.6 broadcast_in_dim.187
  594.4 5.3 collective-permute-done.46
  601.9 5.3 copy.113
  (230 shorter events, 103.1 us)
Async XLA Ops:
  8.6 27.4 %all-to-all-start = ((f32[17,128,128]{2,0,1:T(8,128)}), f32[17,128,128]{2,0,1:T(8,128)S(1)}, u32[]{:S(2)}, u32[]{:S(2)}) async-start(f32[17,128,128]{2,0,1:T(8,128)} %copy.90), calls=%async_computation | async-start | bytes 3145728 | tf_op jit(solution)/shard_map/all_to_all | solution.py:345
  37.2 25.2 %collective-permute-start.1 = (f32[128,16,128]{2,1,0:T(8,128)S(1)}, f32[128,16,128]{2,1,0:T(8,128)S(1)}, u32[]{:S(2)}, u32[]{:S(2)}) collective-permute-start(f32[128,16,128]{2,1,0:T(8,128)S(1)} %bitcast.158), channel_id=1, source_target_pairs={{0,1},{1,2},{2,3},{3,0},{4,5},{5,6},{6,7},{7,4},{8,9},{9,10},{10,1... | collective-permute-start | bytes 3145736 | tf_op jit(solution)/shard_map/ppermute | solution.py:328
  38.5 24.7 %collective-permute-start = (f32[128,16,128]{2,1,0:T(8,128)S(1)}, f32[128,16,128]{2,1,0:T(8,128)S(1)}, u32[]{:S(2)}, u32[]{:S(2)}) collective-permute-start(f32[128,16,128]{2,1,0:T(8,128)S(1)} %bitcast.159), channel_id=1, source_target_pairs={{1,0},{2,1},{3,2},{0,3},{5,4},{6,5},{7,6},{4,7},{9,8},{10,9},{11,1... | collective-permute-start | bytes 3145736 | tf_op jit(solution)/shard_map/ppermute | solution.py:329
  42.3 167.5 %all-to-all-start.1 = ((f32[16,512,128]{2,0,1:T(8,128)}), f32[16,512,128]{2,0,1:T(8,128)}, u32[]{:S(2)}, u32[]{:S(2)}) async-start(f32[16,512,128]{2,0,1:T(8,128)} %bitcast.166), calls=%async_computation.1 | async-start | bytes 8388608 | tf_op jit(solution)/shard_map/all_to_all | solution.py:345
  63.3 13.3 %collective-permute-start.2 = (f32[64,16,128]{2,1,0:T(8,128)}, f32[64,16,128]{2,1,0:T(8,128)}, u32[]{:S(2)}, u32[]{:S(2)}) collective-permute-start(f32[64,16,128]{2,1,0:T(8,128)} %slice.235), channel_id=1, source_target_pairs={{0,1},{1,2},{2,3},{3,0},{4,5},{5,6},{6,7},{7,4},{8,9},{9,10},{10,1... | collective-permute-start | bytes 1572872 | tf_op jit(solution)/shard_map/ppermute | solution.py:330
  64.1 12.5 %collective-permute-start.3 = (f32[64,16,128]{2,1,0:T(8,128)}, f32[64,16,128]{2,1,0:T(8,128)}, u32[]{:S(2)}, u32[]{:S(2)}) collective-permute-start(f32[64,16,128]{2,1,0:T(8,128)} %slice.236), channel_id=1, source_target_pairs={{1,0},{2,1},{3,2},{0,3},{5,4},{6,5},{7,6},{4,7},{9,8},{10,9},{11,1... | collective-permute-start | bytes 1572872 | tf_op jit(solution)/shard_map/ppermute | solution.py:331
  66.8 24.8 %copy-start.12 = (s32[4]{0:T(128)}, s32[4]{0:T(128)S(1)}, u32[]{:S(2)}) copy-start(s32[4]{0:T(128)S(1)} %fusion.30.at_ref) | copy-start | bytes 52
  83.0 19.6 %collective-permute-start.4 = (f32[16,64,128]{2,1,0:T(8,128)}, f32[16,64,128]{2,1,0:T(8,128)S(1)}, u32[]{:S(2)}, u32[]{:S(2)}) collective-permute-start(f32[16,64,128]{2,1,0:T(8,128)} %get-tuple-element.45), channel_id=1, source_target_pairs={{0,32},{4,36},{8,40},{12,44},{16,48},{20,52},{24,56},{28,60},{32,6... | collective-permute-start | bytes 1572872 | tf_op jit(solution)/shard_map/ppermute | solution.py:351
  96.0 60.8 %collective-permute-start.10 = (f32[128,16,128]{2,1,0:T(8,128)}, f32[128,16,128]{2,1,0:T(8,128)S(1)}, u32[]{:S(2)}, u32[]{:S(2)}) collective-permute-start(f32[128,16,128]{2,1,0:T(8,128)} %get-tuple-element.100), channel_id=1, source_target_pairs={{0,64},{4,96},{8,0},{12,32},{16,68},{20,100},{24,4},{28,36},{32,10... | collective-permute-start | bytes 3145736 | tf_op jit(solution)/shard_map/ppermute | solution.py:391
  101.1 39.7 %collective-permute-start.5 = (f32[16,64,128]{2,1,0:T(8,128)S(1)}, f32[16,64,128]{2,1,0:T(8,128)S(1)}, u32[]{:S(2)}, u32[]{:S(2)}) collective-permute-start(f32[16,64,128]{2,1,0:T(8,128)S(1)} %copy-done.19), channel_id=1, source_target_pairs={{32,0},{36,4},{40,8},{44,12},{48,16},{52,20},{56,24},{60,28},{64,3... | collective-permute-start | bytes 1572872 | tf_op jit(solution)/shard_map/ppermute | solution.py:352
  102.5 61.0 %copy-start.26 = (bf16[2,384,128]{2,1,0:T(8,128)(2,1)S(1)}, bf16[2,384,128]{2,1,0:T(8,128)(2,1)}, u32[]{:S(2)}) copy-start(bf16[2,384,128]{2,1,0:T(8,128)(2,1)} %pad_maximum_fusion.14) | copy-start | bytes 589828
  102.5 49.0 %copy-start.6 = (f32[16,64,128]{2,1,0:T(8,128)}, f32[16,64,128]{2,1,0:T(8,128)S(1)}, u32[]{:S(2)}) copy-start(f32[16,64,128]{2,1,0:T(8,128)S(1)} %collective-permute-done.4.zb_ref) | copy-start | bytes 1572868
  142.8 70.6 %collective-permute-start.7 = (f32[160,16,128]{2,1,0:T(8,128)}, f32[160,16,128]{2,1,0:T(8,128)}, u32[]{:S(2)}, u32[]{:S(2)}) collective-permute-start(f32[160,16,128]{2,1,0:T(8,128)} %pad_maximum_fusion.1), channel_id=1, source_target_pairs={{4,0},{8,4},{12,8},{16,12},{20,16},{24,20},{28,24},{36,32},{40,36}... | collective-permute-start | bytes 3932168 | tf_op jit(solution)/shard_map/ppermute | solution.py:358
  146.4 67.0 %collective-permute-start.6 = (f32[160,16,128]{2,1,0:T(8,128)}, f32[160,16,128]{2,1,0:T(8,128)}, u32[]{:S(2)}, u32[]{:S(2)}) collective-permute-start(f32[160,16,128]{2,1,0:T(8,128)} %pad_maximum_fusion), channel_id=1, source_target_pairs={{0,4},{4,8},{8,12},{12,16},{16,20},{20,24},{24,28},{32,36},{36,40}... | collective-permute-start | bytes 3932168 | tf_op jit(solution)/shard_map/ppermute | solution.py:357
  151.5 50.4 %collective-permute-start.11 = (f32[128,16,128]{2,1,0:T(8,128)}, f32[128,16,128]{2,1,0:T(8,128)S(1)}, u32[]{:S(2)}, u32[]{:S(2)}) collective-permute-start(f32[128,16,128]{2,1,0:T(8,128)} %get-tuple-element.99), channel_id=1, source_target_pairs={{0,96},{4,0},{8,32},{12,64},{16,100},{20,4},{24,36},{28,68},{32,8}... | collective-permute-start | bytes 3145736 | tf_op jit(solution)/shard_map/ppermute | solution.py:391
  153.8 49.9 %collective-permute-start.8 = (f32[128,16,128]{2,1,0:T(8,128)}, f32[128,16,128]{2,1,0:T(8,128)}, u32[]{:S(2)}, u32[]{:S(2)}) collective-permute-start(f32[128,16,128]{2,1,0:T(8,128)} %get-tuple-element.102), channel_id=1, source_target_pairs={{0,0},{4,32},{8,64},{12,96},{16,4},{20,36},{24,68},{28,100},{32,40... | collective-permute-start | bytes 3145736 | tf_op jit(solution)/shard_map/ppermute | solution.py:391
  156.8 46.9 %collective-permute-start.9 = (f32[128,16,128]{2,1,0:T(8,128)}, f32[128,16,128]{2,1,0:T(8,128)}, u32[]{:S(2)}, u32[]{:S(2)}) collective-permute-start(f32[128,16,128]{2,1,0:T(8,128)} %get-tuple-element.101), channel_id=1, source_target_pairs={{0,32},{4,64},{8,96},{12,0},{16,36},{20,68},{24,100},{28,4},{32,72... | collective-permute-start | bytes 3145736 | tf_op jit(solution)/shard_map/ppermute | solution.py:391
  213.4 14.0 %copy-start = (f32[8,16,64,128]{3,2,1,0:T(8,128)}, f32[8,16,64,128]{3,2,1,0:T(8,128)S(1)}, u32[]{:S(2)}) copy-start(f32[8,16,64,128]{3,2,1,0:T(8,128)S(1)} %copy.108) | copy-start | bytes 12582916
  213.5 16.5 %copy-start.16 = (f32[128,64,128]{2,1,0:T(8,128)S(1)}, f32[128,64,128]{2,1,0:T(8,128)}, u32[]{:S(2)}) copy-start(f32[128,64,128]{2,1,0:T(8,128)} %copy-done.15) | copy-start | bytes 12582916
  227.3 24.6 %collective-permute-start.16 = (f32[16,64,128]{2,1,0:T(8,128)S(1)}, f32[16,64,128]{2,1,0:T(8,128)S(1)}, u32[]{:S(2)}, u32[]{:S(2)}) collective-permute-start(f32[16,64,128]{2,1,0:T(8,128)S(1)} %get-tuple-element.57), channel_id=1, source_target_pairs={{0,32},{4,36},{8,40},{12,44},{16,48},{20,52},{24,56},{28,60},{32,6... | collective-permute-start | bytes 1572872 | tf_op jit(solution)/shard_map/ppermute | solution.py:351
  228.7 23.3 %collective-permute-start.17 = (f32[16,64,128]{2,1,0:T(8,128)S(1)}, f32[16,64,128]{2,1,0:T(8,128)S(1)}, u32[]{:S(2)}, u32[]{:S(2)}) collective-permute-start(f32[16,64,128]{2,1,0:T(8,128)S(1)} %get-tuple-element.58), channel_id=1, source_target_pairs={{32,0},{36,4},{40,8},{44,12},{48,16},{52,20},{56,24},{60,28},{64,3... | collective-permute-start | bytes 1572872 | tf_op jit(solution)/shard_map/ppermute | solution.py:352
  230.0 21.8 %copy-start.29 = (bf16[2,64,96]{2,1,0:T(8,128)(2,1)S(1)}, bf16[2,64,96]{2,1,0:T(8,128)(2,1)}, u32[]{:S(2)}) copy-start(bf16[2,64,96]{2,1,0:T(8,128)(2,1)} %get-tuple-element.135) | copy-start | bytes 73732
  230.0 21.8 %copy-start.30 = (bf16[2,64,96]{2,1,0:T(8,128)(2,1)S(1)}, bf16[2,64,96]{2,1,0:T(8,128)(2,1)}, u32[]{:S(2)}) copy-start(bf16[2,64,96]{2,1,0:T(8,128)(2,1)} %get-tuple-element.136) | copy-start | bytes 73732
  230.0 21.9 %copy-start.25 = (bf16[2,128,480]{2,1,0:T(8,128)(2,1)S(1)}, bf16[2,128,480]{2,1,0:T(8,128)(2,1)}, u32[]{:S(2)}) copy-start(bf16[2,128,480]{2,1,0:T(8,128)(2,1)} %pad_maximum_fusion.11) | copy-start | bytes 737284
  242.4 21.2 %collective-permute-start.12 = (f32[16,64,128]{2,1,0:T(8,128)S(1)}, f32[16,64,128]{2,1,0:T(8,128)S(1)}, u32[]{:S(2)}, u32[]{:S(2)}) collective-permute-start(f32[16,64,128]{2,1,0:T(8,128)S(1)} %get-tuple-element.50), channel_id=1, source_target_pairs={{0,32},{4,36},{8,40},{12,44},{16,48},{20,52},{24,56},{28,60},{32,6... | collective-permute-start | bytes 1572872 | tf_op jit(solution)/shard_map/ppermute | solution.py:351
  250.5 13.1 %collective-permute-start.13 = (f32[16,64,128]{2,1,0:T(8,128)S(1)}, f32[16,64,128]{2,1,0:T(8,128)S(1)}, u32[]{:S(2)}, u32[]{:S(2)}) collective-permute-start(f32[16,64,128]{2,1,0:T(8,128)S(1)} %get-tuple-element.51), channel_id=1, source_target_pairs={{32,0},{36,4},{40,8},{44,12},{48,16},{52,20},{56,24},{60,28},{64,3... | collective-permute-start | bytes 1572872 | tf_op jit(solution)/shard_map/ppermute | solution.py:352
  258.3 21.2 %collective-permute-start.18 = (f32[128,16,128]{2,1,0:T(8,128)}, f32[128,16,128]{2,1,0:T(8,128)}, u32[]{:S(2)}, u32[]{:S(2)}) collective-permute-start(f32[128,16,128]{2,1,0:T(8,128)} %get-tuple-element.60), channel_id=1, source_target_pairs={{0,4},{4,8},{8,12},{12,16},{16,20},{20,24},{24,28},{32,36},{36,40}... | collective-permute-start | bytes 3145736 | tf_op jit(solution)/shard_map/ppermute | solution.py:357
  260.2 19.3 %collective-permute-start.19 = (f32[128,16,128]{2,1,0:T(8,128)S(1)}, f32[128,16,128]{2,1,0:T(8,128)}, u32[]{:S(2)}, u32[]{:S(2)}) collective-permute-start(f32[128,16,128]{2,1,0:T(8,128)S(1)} %get-tuple-element.61), channel_id=1, source_target_pairs={{4,0},{8,4},{12,8},{16,12},{20,16},{24,20},{28,24},{36,32},{40,36}... | collective-permute-start | bytes 3145736 | tf_op jit(solution)/shard_map/ppermute | solution.py:358
  263.6 14.5 %copy-start.27 = (bf16[2,128,128]{2,1,0:T(8,128)(2,1)S(1)}, bf16[2,128,128]{2,1,0:T(8,128)(2,1)}, u32[]{:S(2)}) copy-start(bf16[2,128,128]{2,1,0:T(8,128)(2,1)} %get-tuple-element.127) | copy-start | bytes 196612
  263.6 14.5 %copy-start.28 = (bf16[2,128,128]{2,1,0:T(8,128)(2,1)S(1)}, bf16[2,128,128]{2,1,0:T(8,128)(2,1)}, u32[]{:S(2)}) copy-start(bf16[2,128,128]{2,1,0:T(8,128)(2,1)} %get-tuple-element.128) | copy-start | bytes 196612
  270.2 18.9 %collective-permute-start.14 = (f32[128,16,128]{2,1,0:T(8,128)}, f32[128,16,128]{2,1,0:T(8,128)}, u32[]{:S(2)}, u32[]{:S(2)}) collective-permute-start(f32[128,16,128]{2,1,0:T(8,128)} %get-tuple-element.53), channel_id=1, source_target_pairs={{0,4},{4,8},{8,12},{12,16},{16,20},{20,24},{24,28},{32,36},{36,40}... | collective-permute-start | bytes 3145736 | tf_op jit(solution)/shard_map/ppermute | solution.py:357
  276.2 16.5 %collective-permute-start.15 = (f32[128,16,128]{2,1,0:T(8,128)}, f32[128,16,128]{2,1,0:T(8,128)}, u32[]{:S(2)}, u32[]{:S(2)}) collective-permute-start(f32[128,16,128]{2,1,0:T(8,128)} %get-tuple-element.54), channel_id=1, source_target_pairs={{4,0},{8,4},{12,8},{16,12},{20,16},{24,20},{28,24},{36,32},{40,36}... | collective-permute-start | bytes 3145736 | tf_op jit(solution)/shard_map/ppermute | solution.py:358
  278.2 14.5 %slice-start = ((s8[4259840]{0:T(1024)(128)(4,1)}), s8[4194304]{0:T(1024)(128)(4,1)S(1)}, s32[]{:S(2)}) async-start(s8[4259840]{0:T(1024)(128)(4,1)} %bitcast.163), calls=%async_computation.3 | async-start | bytes 8388608
  300.1 10.4 %collective-permute-start.20 = (f32[64,16,128]{2,1,0:T(8,128)S(1)}, f32[64,16,128]{2,1,0:T(8,128)S(1)}, u32[]{:S(2)}, u32[]{:S(2)}) collective-permute-start(f32[64,16,128]{2,1,0:T(8,128)S(1)} %get-tuple-element.95), channel_id=1, source_target_pairs={{0,1},{1,2},{2,3},{3,0},{4,5},{5,6},{6,7},{7,4},{8,9},{9,10},{10,1... | collective-permute-start | bytes 1572872 | tf_op jit(solution)/shard_map/ppermute | solution.py:337
  301.2 9.3 %collective-permute-start.22 = (f32[64,16,128]{2,1,0:T(8,128)S(1)}, f32[64,16,128]{2,1,0:T(8,128)S(1)}, u32[]{:S(2)}, u32[]{:S(2)}) collective-permute-start(f32[64,16,128]{2,1,0:T(8,128)S(1)} %get-tuple-element.96), channel_id=1, source_target_pairs={{1,0},{2,1},{3,2},{0,3},{5,4},{6,5},{7,6},{4,7},{9,8},{10,9},{11,1... | collective-permute-start | bytes 1572872 | tf_op jit(solution)/shard_map/ppermute | solution.py:338
  311.7 20.8 %collective-permute-start.21 = (f32[128,16,128]{2,1,0:T(8,128)}, f32[128,16,128]{2,1,0:T(8,128)}, u32[]{:S(2)}, u32[]{:S(2)}) collective-permute-start(f32[128,16,128]{2,1,0:T(8,128)} %pad_maximum_fusion.6), channel_id=1, source_target_pairs={{0,1},{1,2},{2,3},{3,0},{4,5},{5,6},{6,7},{7,4},{8,9},{9,10},{10,1... | collective-permute-start | bytes 3145736 | tf_op jit(solution)/shard_map/ppermute | solution.py:341
  313.5 20.0 %collective-permute-start.23 = (f32[128,16,128]{2,1,0:T(8,128)}, f32[128,16,128]{2,1,0:T(8,128)S(1)}, u32[]{:S(2)}, u32[]{:S(2)}) collective-permute-start(f32[128,16,128]{2,1,0:T(8,128)} %pad_maximum_fusion.7), channel_id=1, source_target_pairs={{1,0},{2,1},{3,2},{0,3},{5,4},{6,5},{7,6},{4,7},{9,8},{10,9},{11,1... | collective-permute-start | bytes 3145736 | tf_op jit(solution)/shard_map/ppermute | solution.py:341
  315.7 54.6 %copy-start.13 = (s32[4]{0:T(128)S(1)}, s32[4]{0:T(128)}, u32[]{:S(2)}) copy-start(s32[4]{0:T(128)} %copy-done.12) | copy-start | bytes 52
  335.4 22.2 %collective-permute-start.25 = (f32[128,16,128]{2,1,0:T(8,128)S(1)}, f32[128,16,128]{2,1,0:T(8,128)S(1)}, u32[]{:S(2)}, u32[]{:S(2)}) collective-permute-start(f32[128,16,128]{2,1,0:T(8,128)S(1)} %fusion.9.refs_0_), channel_id=1, source_target_pairs={{0,1},{1,2},{2,3},{3,0},{4,5},{5,6},{6,7},{7,4},{8,9},{9,10},{10,1... | collective-permute-start | bytes 3145736 | tf_op jit(solution)/shard_map/ppermute | solution.py:328
  337.2 21.8 %collective-permute-start.24 = (f32[128,16,128]{2,1,0:T(8,128)S(1)}, f32[128,16,128]{2,1,0:T(8,128)S(1)}, u32[]{:S(2)}, u32[]{:S(2)}) collective-permute-start(f32[128,16,128]{2,1,0:T(8,128)S(1)} %fusion.9.refs_0_), channel_id=1, source_target_pairs={{1,0},{2,1},{3,2},{0,3},{5,4},{6,5},{7,6},{4,7},{9,8},{10,9},{11,1... | collective-permute-start | bytes 3145736 | tf_op jit(solution)/shard_map/ppermute | solution.py:329
  357.7 12.0 %collective-permute-start.26 = (f32[64,16,128]{2,1,0:T(8,128)S(1)}, f32[64,16,128]{2,1,0:T(8,128)S(1)}, u32[]{:S(2)}, u32[]{:S(2)}) collective-permute-start(f32[64,16,128]{2,1,0:T(8,128)S(1)} %slice.254), channel_id=1, source_target_pairs={{0,1},{1,2},{2,3},{3,0},{4,5},{5,6},{6,7},{7,4},{8,9},{9,10},{10,1... | collective-permute-start | bytes 1572872 | tf_op jit(solution)/shard_map/ppermute | solution.py:330
  359.1 11.2 %collective-permute-start.27 = (f32[64,16,128]{2,1,0:T(8,128)S(1)}, f32[64,16,128]{2,1,0:T(8,128)S(1)}, u32[]{:S(2)}, u32[]{:S(2)}) collective-permute-start(f32[64,16,128]{2,1,0:T(8,128)S(1)} %slice.255), channel_id=1, source_target_pairs={{1,0},{2,1},{3,2},{0,3},{5,4},{6,5},{7,6},{4,7},{9,8},{10,9},{11,1... | collective-permute-start | bytes 1572872 | tf_op jit(solution)/shard_map/ppermute | solution.py:331
  371.8 13.8 %collective-permute-start.28 = (f32[16,64,128]{2,1,0:T(8,128)S(1)}, f32[16,64,128]{2,1,0:T(8,128)S(1)}, u32[]{:S(2)}, u32[]{:S(2)}) collective-permute-start(f32[16,64,128]{2,1,0:T(8,128)S(1)} %get-tuple-element.63), channel_id=1, source_target_pairs={{0,32},{4,36},{8,40},{12,44},{16,48},{20,52},{24,56},{28,60},{32,6... | collective-permute-start | bytes 1572872 | tf_op jit(solution)/shard_map/ppermute | solution.py:351
  375.8 22.3 %collective-permute-start.29 = (f32[16,64,128]{2,1,0:T(8,128)S(1)}, f32[16,64,128]{2,1,0:T(8,128)S(1)}, u32[]{:S(2)}, u32[]{:S(2)}) collective-permute-start(f32[16,64,128]{2,1,0:T(8,128)S(1)} %get-tuple-element.64), channel_id=1, source_target_pairs={{32,0},{36,4},{40,8},{44,12},{48,16},{52,20},{56,24},{60,28},{64,3... | collective-permute-start | bytes 1572872 | tf_op jit(solution)/shard_map/ppermute | solution.py:352
  377.3 47.6 %copy-start.1 = (f32[8,16,64,128]{3,2,1,0:T(8,128)S(1)}, f32[8,16,64,128]{3,2,1,0:T(8,128)}, u32[]{:S(2)}) copy-start(f32[8,16,64,128]{3,2,1,0:T(8,128)} %copy-done) | copy-start | bytes 12582916
  398.2 25.1 %collective-permute-start.31 = (f32[160,16,128]{2,1,0:T(8,128)S(1)}, f32[160,16,128]{2,1,0:T(8,128)S(1)}, u32[]{:S(2)}, u32[]{:S(2)}) collective-permute-start(f32[160,16,128]{2,1,0:T(8,128)S(1)} %pad_maximum_fusion.3), channel_id=1, source_target_pairs={{4,0},{8,4},{12,8},{16,12},{20,16},{24,20},{28,24},{36,32},{40,36}... | collective-permute-start | bytes 3932168 | tf_op jit(solution)/shard_map/ppermute | solution.py:358
  401.8 38.5 %copy-start.17 = (f32[128,64,128]{2,1,0:T(8,128)S(1)}, f32[128,64,128]{2,1,0:T(8,128)}, u32[]{:S(2)}) copy-start(f32[128,64,128]{2,1,0:T(8,128)} %copy-done.15) | copy-start | bytes 12582916
  401.8 23.1 %collective-permute-start.30 = (f32[160,16,128]{2,1,0:T(8,128)S(1)}, f32[160,16,128]{2,1,0:T(8,128)S(1)}, u32[]{:S(2)}, u32[]{:S(2)}) collective-permute-start(f32[160,16,128]{2,1,0:T(8,128)S(1)} %pad_maximum_fusion.2), channel_id=1, source_target_pairs={{0,4},{4,8},{8,12},{12,16},{16,20},{20,24},{24,28},{32,36},{36,40}... | collective-permute-start | bytes 3932168 | tf_op jit(solution)/shard_map/ppermute | solution.py:357
  435.6 20.7 %collective-permute-start.36 = (f32[16,64,128]{2,1,0:T(8,128)S(1)}, f32[16,64,128]{2,1,0:T(8,128)S(1)}, u32[]{:S(2)}, u32[]{:S(2)}) collective-permute-start(f32[16,64,128]{2,1,0:T(8,128)S(1)} %get-tuple-element.72), channel_id=1, source_target_pairs={{0,32},{4,36},{8,40},{12,44},{16,48},{20,52},{24,56},{28,60},{32,6... | collective-permute-start | bytes 1572872 | tf_op jit(solution)/shard_map/ppermute | solution.py:351
  439.0 17.3 %collective-permute-start.37 = (f32[16,64,128]{2,1,0:T(8,128)S(1)}, f32[16,64,128]{2,1,0:T(8,128)S(1)}, u32[]{:S(2)}, u32[]{:S(2)}) collective-permute-start(f32[16,64,128]{2,1,0:T(8,128)S(1)} %get-tuple-element.73), channel_id=1, source_target_pairs={{32,0},{36,4},{40,8},{44,12},{48,16},{52,20},{56,24},{60,28},{64,3... | collective-permute-start | bytes 1572872 | tf_op jit(solution)/shard_map/ppermute | solution.py:352
  451.0 15.6 %collective-permute-start.32 = (f32[16,64,128]{2,1,0:T(8,128)S(1)}, f32[16,64,128]{2,1,0:T(8,128)S(1)}, u32[]{:S(2)}, u32[]{:S(2)}) collective-permute-start(f32[16,64,128]{2,1,0:T(8,128)S(1)} %get-tuple-element.66), channel_id=1, source_target_pairs={{0,32},{4,36},{8,40},{12,44},{16,48},{20,52},{24,56},{28,60},{32,6... | collective-permute-start | bytes 1572872 | tf_op jit(solution)/shard_map/ppermute | solution.py:351
  455.0 11.6 %collective-permute-start.33 = (f32[16,64,128]{2,1,0:T(8,128)S(1)}, f32[16,64,128]{2,1,0:T(8,128)S(1)}, u32[]{:S(2)}, u32[]{:S(2)}) collective-permute-start(f32[16,64,128]{2,1,0:T(8,128)S(1)} %get-tuple-element.67), channel_id=1, source_target_pairs={{32,0},{36,4},{40,8},{44,12},{48,16},{52,20},{56,24},{60,28},{64,3... | collective-permute-start | bytes 1572872 | tf_op jit(solution)/shard_map/ppermute | solution.py:352
  459.4 21.4 %collective-permute-start.38 = (f32[128,16,128]{2,1,0:T(8,128)S(1)}, f32[128,16,128]{2,1,0:T(8,128)S(1)}, u32[]{:S(2)}, u32[]{:S(2)}) collective-permute-start(f32[128,16,128]{2,1,0:T(8,128)S(1)} %get-tuple-element.75), channel_id=1, source_target_pairs={{0,4},{4,8},{8,12},{12,16},{16,20},{20,24},{24,28},{32,36},{36,40}... | collective-permute-start | bytes 3145736 | tf_op jit(solution)/shard_map/ppermute | solution.py:357
  464.7 16.2 %collective-permute-start.39 = (f32[128,16,128]{2,1,0:T(8,128)S(1)}, f32[128,16,128]{2,1,0:T(8,128)S(1)}, u32[]{:S(2)}, u32[]{:S(2)}) collective-permute-start(f32[128,16,128]{2,1,0:T(8,128)S(1)} %get-tuple-element.76), channel_id=1, source_target_pairs={{4,0},{8,4},{12,8},{16,12},{20,16},{24,20},{28,24},{36,32},{40,36}... | collective-permute-start | bytes 3145736 | tf_op jit(solution)/shard_map/ppermute | solution.py:358
  469.7 20.9 %collective-permute-start.34 = (f32[128,16,128]{2,1,0:T(8,128)S(1)}, f32[128,16,128]{2,1,0:T(8,128)S(1)}, u32[]{:S(2)}, u32[]{:S(2)}) collective-permute-start(f32[128,16,128]{2,1,0:T(8,128)S(1)} %get-tuple-element.69), channel_id=1, source_target_pairs={{0,4},{4,8},{8,12},{12,16},{16,20},{20,24},{24,28},{32,36},{36,40}... | collective-permute-start | bytes 3145736 | tf_op jit(solution)/shard_map/ppermute | solution.py:357
  478.9 16.4 %collective-permute-start.35 = (f32[128,16,128]{2,1,0:T(8,128)S(1)}, f32[128,16,128]{2,1,0:T(8,128)S(1)}, u32[]{:S(2)}, u32[]{:S(2)}) collective-permute-start(f32[128,16,128]{2,1,0:T(8,128)S(1)} %get-tuple-element.70), channel_id=1, source_target_pairs={{4,0},{8,4},{12,8},{16,12},{20,16},{24,20},{28,24},{36,32},{40,36}... | collective-permute-start | bytes 3145736 | tf_op jit(solution)/shard_map/ppermute | solution.py:358
  501.8 15.2 %collective-permute-start.40 = (f32[64,16,128]{2,1,0:T(8,128)S(1)}, f32[64,16,128]{2,1,0:T(8,128)S(1)}, u32[]{:S(2)}, u32[]{:S(2)}) collective-permute-start(f32[64,16,128]{2,1,0:T(8,128)S(1)} %get-tuple-element.87), channel_id=1, source_target_pairs={{0,1},{1,2},{2,3},{3,0},{4,5},{5,6},{6,7},{7,4},{8,9},{9,10},{10,1... | collective-permute-start | bytes 1572872 | tf_op jit(solution)/shard_map/ppermute | solution.py:337
  501.9 15.1 %collective-permute-start.42 = (f32[64,16,128]{2,1,0:T(8,128)S(1)}, f32[64,16,128]{2,1,0:T(8,128)S(1)}, u32[]{:S(2)}, u32[]{:S(2)}) collective-permute-start(f32[64,16,128]{2,1,0:T(8,128)S(1)} %get-tuple-element.88), channel_id=1, source_target_pairs={{1,0},{2,1},{3,2},{0,3},{5,4},{6,5},{7,6},{4,7},{9,8},{10,9},{11,1... | collective-permute-start | bytes 1572872 | tf_op jit(solution)/shard_map/ppermute | solution.py:338
  517.2 15.6 %collective-permute-start.41 = (f32[128,16,128]{2,1,0:T(8,128)S(1)}, f32[128,16,128]{2,1,0:T(8,128)S(1)}, u32[]{:S(2)}, u32[]{:S(2)}) collective-permute-start(f32[128,16,128]{2,1,0:T(8,128)S(1)} %pad_maximum_fusion.9), channel_id=1, source_target_pairs={{0,1},{1,2},{2,3},{3,0},{4,5},{5,6},{6,7},{7,4},{8,9},{9,10},{10,1... | collective-permute-start | bytes 3145736 | tf_op jit(solution)/shard_map/ppermute | solution.py:341
  517.8 15.1 %collective-permute-start.43 = (f32[128,16,128]{2,1,0:T(8,128)S(1)}, f32[128,16,128]{2,1,0:T(8,128)S(1)}, u32[]{:S(2)}, u32[]{:S(2)}) collective-permute-start(f32[128,16,128]{2,1,0:T(8,128)S(1)} %pad_maximum_fusion.10), channel_id=1, source_target_pairs={{1,0},{2,1},{3,2},{0,3},{5,4},{6,5},{7,6},{4,7},{9,8},{10,9},{11,1... | collective-permute-start | bytes 3145736 | tf_op jit(solution)/shard_map/ppermute | solution.py:341
  561.3 25.4 %collective-permute-start.45 = (f32[16,8,16,128]{3,2,1,0:T(8,128)}, f32[16,8,16,128]{3,2,1,0:T(8,128)S(1)}, u32[]{:S(2)}, u32[]{:S(2)}) collective-permute-start(f32[16,8,16,128]{3,2,1,0:T(8,128)} %bitcast.157), channel_id=1, source_target_pairs={{0,1},{1,2},{2,3},{3,0},{4,5},{5,6},{6,7},{7,4},{8,9},{9,10},{10,1... | collective-permute-start | bytes 3145736 | tf_op jit(solution)/shard_map/ppermute | solution.py:328
  562.1 24.7 %collective-permute-start.44 = (f32[16,8,16,128]{3,2,1,0:T(8,128)}, f32[16,8,16,128]{3,2,1,0:T(8,128)S(1)}, u32[]{:S(2)}, u32[]{:S(2)}) collective-permute-start(f32[16,8,16,128]{3,2,1,0:T(8,128)} %bitcast.157), channel_id=1, source_target_pairs={{1,0},{2,1},{3,2},{0,3},{5,4},{6,5},{7,6},{4,7},{9,8},{10,9},{11,1... | collective-permute-start | bytes 3145736 | tf_op jit(solution)/shard_map/ppermute | solution.py:329
  586.7 13.0 %collective-permute-start.46 = (f32[8,8,16,128]{3,2,1,0:T(8,128)S(1)}, f32[8,8,16,128]{3,2,1,0:T(8,128)S(1)}, u32[]{:S(2)}, u32[]{:S(2)}) collective-permute-start(f32[8,8,16,128]{3,2,1,0:T(8,128)S(1)} %slice.267), channel_id=1, source_target_pairs={{0,1},{1,2},{2,3},{3,0},{4,5},{5,6},{6,7},{7,4},{8,9},{9,10},{10,1... | collective-permute-start | bytes 1572872 | tf_op jit(solution)/shard_map/ppermute | solution.py:330
  586.8 12.9 %collective-permute-start.47 = (f32[8,8,16,128]{3,2,1,0:T(8,128)S(1)}, f32[8,8,16,128]{3,2,1,0:T(8,128)S(1)}, u32[]{:S(2)}, u32[]{:S(2)}) collective-permute-start(f32[8,8,16,128]{3,2,1,0:T(8,128)S(1)} %slice.268), channel_id=1, source_target_pairs={{1,0},{2,1},{3,2},{0,3},{5,4},{6,5},{7,6},{4,7},{9,8},{10,9},{11,1... | collective-permute-start | bytes 1572872 | tf_op jit(solution)/shard_map/ppermute | solution.py:331
  (22 other events, 101.9 us)
